TPU v7x, 32 devices: a whole 2x2x4 slice. The times are simulated.
32 devices in a mesh: dp: 16 (over z, y, x), tensor: 2 (over core).
Axes of the slice: x: 2, y: 2, z: 4, core: 2. Of those that a mesh axis runs over, the one named last changes fastest.
Arguments:
- tokens: bfloat16 [32768, 768], P('dp'), may hold values from -6.25 to 6.25, as said below
- long_lengths: int32 [32], P('dp'), may hold values from 128 to 512, as said below
- short_lengths: int32 [64], P('dp'), may hold values from 64 to 256, as said below
- query_weight: bfloat16 [768, 768], P(None, 'tensor'), may hold values from -0.21875 to 0.21875
- query_bias: float32 [768], P('tensor'), may hold values from -3 to 3
- key_weight: bfloat16 [768, 768], P(None, 'tensor'), may hold values from -0.21875 to 0.21875
- value_weight: bfloat16 [768, 768], P(None, 'tensor'), may hold values from -0.21875 to 0.21875
- value_bias: float32 [768], P('tensor'), may hold values from -3 to 3
- output_weight: bfloat16 [768, 768], P('tensor'), may hold values from -0.875 to 0.875
- output_bias: float32 [768], replicated, may hold values from -3 to 3
- first_gain: float32 [768], replicated, may hold values from 0.25 to 1.75
- first_shift: float32 [768], replicated, may hold values from -3 to 3
- inner_weight: bfloat16 [768, 3072], P(None, 'tensor'), may hold values from -0.21875 to 0.21875
- inner_bias: float32 [3072], P('tensor'), may hold values from -3 to 3
- outer_weight: bfloat16 [3072, 768], P('tensor'), may hold values from -0.109375 to 0.109375
- outer_bias: float32 [768], replicated, may hold values from -3 to 3
- second_gain: float32 [768], replicated, may hold values from 0.25 to 1.75
- second_shift: float32 [768], replicated, may hold values from -3 to 3
- out_grad: bfloat16 [32768, 768], P('dp'), may hold values from -6 to 6
Outputs:
- block_out: bfloat16 [32768, 768], P('dp')
- tokens_grad: bfloat16 [32768, 768], P('dp')
- query_weight_grad: float32 [768, 768], P('dp', 'tensor')
- query_bias_grad: float32 [768], P('tensor')
- key_weight_grad: float32 [768, 768], P('dp', 'tensor')
- value_weight_grad: float32 [768, 768], P('dp', 'tensor')
- value_bias_grad: float32 [768], P('tensor')
- output_weight_grad: float32 [768, 768], P('tensor', 'dp')
- output_bias_grad: float32 [768], replicated
- first_gain_grad: float32 [768], replicated
- first_shift_grad: float32 [768], replicated
- inner_weight_grad: float32 [768, 3072], P('dp', 'tensor')
- inner_bias_grad: float32 [3072], P('tensor')
- outer_weight_grad: float32 [3072, 768], P('tensor', 'dp')
- outer_bias_grad: float32 [768], replicated
- second_gain_grad: float32 [768], replicated
- second_shift_grad: float32 [768], replicated
- residual_rms: float32 [], replicated
- attention_rms: float32 [], replicated
- feedforward_rms: float32 [], replicated
Inputs may be any that keep to these rules, and one draw needn't show every extreme that they name: `long_lengths`: the entry of a long-bucket sequence; its slot positions from this length on are padding. `short_lengths`: the entry of a short-bucket sequence; its slot positions from this length on are padding. `tokens`: activations of order one.
All inputs are finite; a program needn't handle non-finite values.
Results may differ from a plain program's by a relative error of at most 0.02.
Values may be sent and summed in bfloat16 or wider, within the bound.
No kernel may reach another device: no remote copies, remote signals or barrier semaphores. Data moves between devices by JAX's collectives and lax.ppermute only.
A program may use at most 192 MiB of HBM per device.

v0:
```python
import jax
import jax.numpy as jnp
from jax import lax
from jax.experimental import pallas as pl
from jax.experimental.pallas import tpu as pltpu
from jax.sharding import PartitionSpec as P

D = 768
LONG = 512
SHORT = 256
eps_norm = 1e-05
bf = jnp.bfloat16
f32 = jnp.float32
shape = jax.ShapeDtypeStruct


def nt(a, b):
    return lax.dot_general(a, b, (((1,), (1,)), ((), ())), preferred_element_type=f32)


def nn(a, b):
    return lax.dot_general(a, b, (((1,), (0,)), ((), ())), preferred_element_type=f32)


def tn(a, b):
    return lax.dot_general(a, b, (((0,), (0,)), ((), ())), preferred_element_type=f32)


def whole(dims):
    return pl.BlockSpec(dims, lambda *_: (0,) * len(dims))


def anywhere():
    return pl.BlockSpec(memory_space=pl.ANY)


def settings(flops, mebibytes):
    return dict(
        compiler_params=pltpu.CompilerParams(vmem_limit_bytes=mebibytes << 20),
        cost_estimate=pl.CostEstimate(flops=int(flops), bytes_accessed=int(1e6), transcendentals=0),
    )


def line(ref):
    return ref[...].reshape(1, ref.shape[0])


def slots(rows):
    longs = rows // 2 // LONG
    shorts = rows // 2 // SHORT
    out = [(i * LONG, LONG, i) for i in range(longs)]
    return out + [(rows // 2 + i * SHORT, SHORT, longs + i) for i in range(shorts)]


def slot_length(side_ref, long_ref, short_ref, rows, index):
    longs = rows // 2 // LONG
    shorts = rows // 2 // SHORT
    if index < longs:
        return long_ref[side_ref[0] * longs + index]
    return short_ref[side_ref[0] * shorts + index - longs]


def place_rows(ref, value, places):
    if places is None:
        ref[...] = value
        return
    size = value.shape[0] // len(places)
    for i, p in enumerate(places):
        ref[p * size : (p + 1) * size, :] = value[i * size : (i + 1) * size, :]


def pair_forward(length, q, k, v, put):
    size = q.shape[0]
    lane = lax.broadcasted_iota(jnp.int32, (size, 128), 1)
    low = lane < 64
    pos = lax.broadcasted_iota(jnp.int32, (size, 128), 0)
    bias = jnp.where(pos < length, 0.0, -1e30).astype(bf)
    one = jnp.ones((), bf)
    zero = jnp.zeros((), bf)
    es = []
    for h in range(2):
        mine = low if h == 0 else ~low
        flag = lane == (64 if h == 0 else 0)
        qh = jnp.where(mine, q, jnp.where(flag, one, zero))
        kh = jnp.where(mine, k, jnp.where(flag, bias, zero))
        s = nt(qh, kh)
        m = jnp.max(s, axis=-1, keepdims=True)
        e = jnp.exp(s - m).astype(bf)
        put(h, e)
        es.append(e)
    here = jnp.where(low, one, zero)
    there = jnp.where(low, zero, one)
    both = [jnp.concatenate([v * here, here], 1), jnp.concatenate([v * there, there], 1)]
    out = nn(jnp.concatenate(es, 1), jnp.concatenate(both, 0))
    inv = 1.0 / out[:, 128:]
    return out[:, :128] * inv, inv


def attention_forward_kernel(
    side_ref, long_ref, short_ref,
    x0, x1, wq0, wq1, wk0, wk1, wv0, wv1, bq0, bq1, bv0, bv1, wo0, wo1, bo_ref, gain_ref, shift_ref,
    qkv_ref, ctx_ref, inv_ref, el_ref, es_ref, xhat_ref, dev_ref, low_ref, sums_ref, acc_ref, all_ref,
):
    step = pl.program_id(0)
    half = x0.shape[0]
    rows = 2 * half
    zero = jnp.zeros((1, 256), f32)
    cols = pl.ds(pl.multiple_of(128 * step, 128), 128)
    weights = jnp.concatenate([w[...] for w in (wq0, wq1, wk0, wk1, wv0, wv1)], 1)
    bias = [b[cols].reshape(1, 128) for b in (bq0, bq1, bv0, bv1)]
    bias = jnp.concatenate(bias[:2] + [zero] + bias[2:], 1)
    for i, x in enumerate((x0, x1)):
        qkv_ref[i * half : (i + 1) * half, :] = (nn(x[...], weights) + bias).astype(bf)
    scale = jnp.asarray(0.125, bf)
    for first, size, index in slots(rows):
        at = pl.ds(first, size)
        length = slot_length(side_ref, long_ref, short_ref, rows, index)
        for p in range(2):
            q = qkv_ref[at, 128 * p : 128 * p + 128] * scale
            k = qkv_ref[at, 256 + 128 * p : 384 + 128 * p]
            v = qkv_ref[at, 512 + 128 * p : 640 + 128 * p]

            def put(h, e, p=p, size=size, index=index):
                if size == LONG:
                    el_ref[0, 4 * index + 2 * p + h] = e
                else:
                    es_ref[0, 4 * (index - half // LONG) + 2 * p + h] = e

            ctx, inv = pair_forward(length, q, k, v, put)
            ctx_ref[at, 128 * p : 128 * p + 128] = ctx.astype(bf)
            inv_ref[at, 128 * p : 128 * p + 128] = inv
    all_ref[:, pl.ds(pl.multiple_of(256 * step, 256), 256)] = ctx_ref[...]

    @pl.when(step == pl.num_programs(0) - 1)
    def _():
        parts = []
        for i in range(0, wo0.shape[0], 128):
            parts += [wo0[i : i + 128, :], wo1[i : i + 128, :]]
        acc_ref[...] = nn(all_ref[...], jnp.concatenate(parts, 0))
        resid = jnp.zeros((1, D), f32)
        attn = jnp.zeros((1, D), f32)
        count = jnp.zeros((), jnp.int32)
        for first, size, index in slots(rows):
            at = pl.ds(first, size)
            length = slot_length(side_ref, long_ref, short_ref, rows, index)
            count += length
            usable = lax.broadcasted_iota(jnp.int32, (size, D), 0) < length
            branch = acc_ref[at, :] + line(bo_ref)
            source = x0[at, :] if first < half else x1[first - half : first - half + size, :]
            total = source.astype(f32) + branch
            resid += jnp.sum(jnp.where(usable, total * total, 0.0), axis=0, keepdims=True)
            attn += jnp.sum(jnp.where(usable, branch * branch, 0.0), axis=0, keepdims=True)
            centred = total - jnp.mean(total, axis=-1, keepdims=True)
            dev = lax.rsqrt(jnp.mean(centred * centred, axis=-1, keepdims=True) + eps_norm)
            xhat = centred * dev
            xhat_ref[at, :] = xhat
            dev_ref[at, :] = jnp.broadcast_to(dev, (size, 128))
            low_ref[at, :] = (xhat * line(gain_ref) + line(shift_ref)).astype(bf)
        count = jnp.full((1, D), count, jnp.int32).astype(f32)
        sums_ref[...] = jnp.concatenate([resid, attn, count, jnp.zeros((5, D), f32)], 0)


def attention_forward(place, tokens, wq, wk, wv, bq, bv, wo, bo, gain, shift):
    half = tokens.shape[0] // 4
    rows = 2 * half
    width = wq[0].shape[1]
    steps = width // 128
    longs = half // LONG
    shorts = half // SHORT
    wide = pl.BlockSpec((D, 128), lambda i, *_: (0, i))

    def part(columns):
        return pl.BlockSpec((rows, columns), lambda i, *_: (0, i))

    return pl.pallas_call(
        attention_forward_kernel,
        out_shape=(
            shape((rows, steps * 768), bf),
            shape((rows, steps * 256), bf),
            shape((rows, steps * 256), f32),
            shape((steps, 4 * longs, LONG, LONG), bf),
            shape((steps, 4 * shorts, SHORT, SHORT), bf),
            shape((rows, D), f32),
            shape((rows, 128), f32),
            shape((rows, D), bf),
            shape((8, D), f32),
        ),
        grid_spec=pltpu.PrefetchScalarGridSpec(
            num_scalar_prefetch=3,
            grid=(steps,),
            in_specs=[
                pl.BlockSpec((half, D), lambda i, side, *_: (side[0], 0)),
                pl.BlockSpec((half, D), lambda i, side, *_: (2 + side[0], 0)),
            ]
            + [wide] * 6
            + [whole((width,))] * 4
            + [whole((width, D))] * 2
            + [whole((D,))] * 3,
            out_specs=[
                part(768),
                part(256),
                part(256),
                pl.BlockSpec((1, 4 * longs, LONG, LONG), lambda i, *_: (i, 0, 0, 0)),
                pl.BlockSpec((1, 4 * shorts, SHORT, SHORT), lambda i, *_: (i, 0, 0, 0)),
                whole((rows, D)),
                whole((rows, 128)),
                whole((rows, D)),
                whole((8, D)),
            ],
            scratch_shapes=[pltpu.VMEM((rows, D), f32), pltpu.VMEM((rows, 2 * width), bf)],
        ),
        name="attention_forward",
        **settings(40e9, 58),
    )(*place, tokens, tokens, *wq, *wk, *wv, *bq, *bv, *wo, bo, gain, shift)


def gelu_parts(v):
    cdf = 0.5 * (1.0 + lax.erf(v * 0.7071067811865476))
    return cdf, v * (0.3989422804014327 * jnp.exp(-0.5 * (v * v)))


def ffn_forward_kernel(
    side_ref, long_ref, short_ref,
    low_ref, wi0, wi1, bi0, bi1, wo0, wo1, xhat_hbm, grad_hbm, gain1_ref, shift1_ref, bo_ref, gain_ref, shift_ref,
    act0, slope0, slope1, out_hbm, back_hbm, low_hbm, other_ref, sums_ref,
    acc_ref, act1, xhat_ref, grad_ref, out_ref, back_low, in_sem, out_sem, *, chunk, places,
):
    step = pl.program_id(0)
    rows = low_ref.shape[0]
    half = rows // 2
    width = wi0.shape[1]
    fetches = [pltpu.make_async_copy(xhat_hbm, xhat_ref, in_sem.at[0])]
    for i in range(2):
        source = grad_hbm.at[pl.ds(pl.multiple_of((2 * i + side_ref[0]) * half, half), half), :]
        fetches.append(pltpu.make_async_copy(source, grad_ref.at[i * half : (i + 1) * half, :], in_sem.at[1 + i]))

    @pl.when(step == 0)
    def _():
        for fetch in fetches:
            fetch.start()

    cols = pl.ds(pl.multiple_of(width * step, width), width)
    win = jnp.concatenate([wi0[...], wi1[...]], 1)
    bias = jnp.concatenate([b[cols].reshape(1, width) for b in (bi0, bi1)], 1)
    wout = jnp.concatenate([wo0[...], wo1[...]], 0)
    for first in range(0, rows, chunk):
        at = pl.ds(first, chunk)
        inner = nn(low_ref[at, :], win) + bias
        cdf, bell = gelu_parts(inner)
        active = (inner * cdf).astype(bf)
        slope = (cdf + bell).astype(bf)
        act0[at, :] = active[:, :width]
        act1[at, cols] = active[:, width:]
        slope0[at, :] = slope[:, :width]
        slope1[at, :] = slope[:, width:]
        part = nn(active, wout)

        @pl.when(step == 0)
        def _():
            acc_ref[at, :] = part

        @pl.when(step > 0)
        def _():
            acc_ref[at, :] += part

    @pl.when(step == pl.num_programs(0) - 1)
    def _():
        for fetch in fetches:
            fetch.wait()
        ffn_sum = jnp.zeros((1, D), f32)
        gain_sum = jnp.zeros((1, D), f32)
        shift_sum = jnp.zeros((1, D), f32)
        bias_sum = jnp.zeros((1, D), f32)
        stores = []
        for i, (first, size, index) in enumerate(slots(rows)):
            at = pl.ds(first, size)
            length = slot_length(side_ref, long_ref, short_ref, rows, index)
            usable = lax.broadcasted_iota(jnp.int32, (size, D), 0) < length
            ffn = acc_ref[at, :] + line(bo_ref)
            ffn_sum += jnp.sum(jnp.where(usable, ffn * ffn, 0.0), axis=0, keepdims=True)
            total = xhat_ref[at, :] * line(gain1_ref) + line(shift1_ref) + ffn
            centred = total - jnp.mean(total, axis=-1, keepdims=True)
            dev = lax.rsqrt(jnp.mean(centred * centred, axis=-1, keepdims=True) + eps_norm)
            xhat = centred * dev
            out_ref[at, :] = (xhat * line(gain_ref) + line(shift_ref)).astype(bf)
            cot = jnp.where(usable, grad_ref[at, :].astype(f32), 0.0)
            gain_sum += jnp.sum(cot * xhat, axis=0, keepdims=True)
            shift_sum += jnp.sum(cot, axis=0, keepdims=True)
            u = cot * line(gain_ref)
            slant = jnp.mean(u * xhat, axis=-1, keepdims=True)
            back = dev * (u - jnp.mean(u, axis=-1, keepdims=True) - xhat * slant)
            bias_sum += jnp.sum(back, axis=0, keepdims=True)
            acc_ref[at, :] = back
            back_low[at, :] = back.astype(bf)
            for j, (source, target) in enumerate(((out_ref, out_hbm), (acc_ref, back_hbm), (back_low, low_hbm))):
                store = pltpu.make_async_copy(source.at[at, :], target.at[at, :], out_sem.at[3 * i + j])
                store.start()
                stores.append(store)
        sums_ref[...] = jnp.concatenate([ffn_sum, gain_sum, shift_sum, bias_sum, jnp.zeros((4, D), f32)], 0)
        place_rows(other_ref, tn(back_low[...], act1[...]).astype(bf), places)
        for store in stores:
            store.wait()


def ffn_forward(place, low, wi, bi, wo, xhat, grad, gain1, shift1, bo, gain, shift, places, width=512, chunk=512):
    rows = low.shape[0]
    half = wi[0].shape[1]
    cols = pl.BlockSpec((D, width), lambda i, *_: (0, i))
    tall = pl.BlockSpec((width, D), lambda i, *_: (i, 0))
    act = pl.BlockSpec((rows, width), lambda i, *_: (0, i))
    row = whole((D,))
    count = len(slots(rows))
    return pl.pallas_call(
        lambda *refs: ffn_forward_kernel(*refs, chunk=chunk, places=places),
        out_shape=(shape((rows, half), bf),) * 3
        + (shape((rows, D), bf), shape((rows, D), f32), shape((rows, D), bf), shape((D, half), bf), shape((8, D), f32)),
        grid_spec=pltpu.PrefetchScalarGridSpec(
            num_scalar_prefetch=3,
            grid=(half // width,),
            in_specs=[whole((rows, D)), cols, cols, whole((half,)), whole((half,)), tall, tall, anywhere(), anywhere()] + [row] * 5,
            out_specs=[act] * 3 + [anywhere()] * 3 + [whole((D, half)), whole((8, D))],
            scratch_shapes=[
                pltpu.VMEM((rows, D), f32),
                pltpu.VMEM((rows, half), bf),
                pltpu.VMEM((rows, D), f32),
                pltpu.VMEM((rows, D), bf),
                pltpu.VMEM((rows, D), bf),
                pltpu.VMEM((rows, D), bf),
                pltpu.SemaphoreType.DMA((3,)),
                pltpu.SemaphoreType.DMA((3 * count,)),
            ],
        ),
        name="ffn_forward",
        **settings(40e9, 58),
    )(*place, low, *wi, *bi, *wo, xhat, grad, gain1, shift1, bo, gain, shift)


def outer_weight_kernel(low_ref, act_ref, out_ref, *, places):
    place_rows(out_ref, tn(low_ref[...], act_ref[...]).astype(bf), places)


def outer_weight(low, act, places, width=512):
    rows, half = act.shape
    return pl.pallas_call(
        lambda *refs: outer_weight_kernel(*refs, places=places),
        out_shape=shape((D, half), bf),
        grid=(half // width,),
        in_specs=[whole((rows, D)), pl.BlockSpec((rows, width), lambda i: (0, i))],
        out_specs=pl.BlockSpec((D, width), lambda i: (0, i)),
        name="outer_weight",
        **settings(10e9, 8),
    )(low, act)


def ffn_backward_kernel(
    back_low, slope0, slope1, wo0, wo1, wi0, wi1, low_ref, back_hbm, xhat_hbm, dev_ref, gain_ref,
    own_ref, other_ref, bias0, bias1, first_hbm, low_hbm, sums_ref,
    inner_ref, acc_ref, xhat_ref, first_low, in_sem, out_sem, *, chunk, places,
):
    step = pl.program_id(0)
    rows = low_ref.shape[0]
    half = wi0.shape[1]
    fetches = [
        pltpu.make_async_copy(back_hbm, acc_ref, in_sem.at[0]),
        pltpu.make_async_copy(xhat_hbm, xhat_ref, in_sem.at[1]),
    ]

    @pl.when(step == 0)
    def _():
        for fetch in fetches:
            fetch.start()

    wout = jnp.concatenate([wo0[...], wo1[...]], 0)
    win = jnp.concatenate([wi0[...], wi1[...]], 1)
    total = jnp.zeros((1, 2 * half), f32)
    for first in range(0, rows, chunk):
        at = pl.ds(first, chunk)
        slope = jnp.concatenate([slope0[at, :], slope1[at, :]], 1).astype(f32)
        inner = (nt(back_low[at, :], wout) * slope).astype(bf)
        total += jnp.sum(inner.astype(f32), axis=0, keepdims=True)
        inner_ref[at, :] = inner
    bias0[...] = jnp.broadcast_to(total[:, :half], bias0.shape)
    bias1[...] = jnp.broadcast_to(total[:, half:], bias1.shape)
    place_rows(own_ref, tn(low_ref[...], inner_ref[:, :half]).astype(bf), places)
    place_rows(other_ref, tn(low_ref[...], inner_ref[:, half:]).astype(bf), places)

    @pl.when(step == 0)
    def _():
        for fetch in fetches:
            fetch.wait()

    for first in range(0, rows, chunk):
        at = pl.ds(first, chunk)
        acc_ref[at, :] += nt(inner_ref[at, :], win)

    @pl.when(step == pl.num_programs(0) - 1)
    def _():
        gain_sum = jnp.zeros((1, D), f32)
        shift_sum = jnp.zeros((1, D), f32)
        bias_sum = jnp.zeros((1, D), f32)
        stores = []
        for i, first in enumerate(range(0, rows, chunk)):
            at = pl.ds(first, chunk)
            grad = acc_ref[at, :]
            xhat = xhat_ref[at, :]
            gain_sum += jnp.sum(grad * xhat, axis=0, keepdims=True)
            shift_sum += jnp.sum(grad, axis=0, keepdims=True)
            u = grad * line(gain_ref)
            slant = jnp.mean(u * xhat, axis=-1, keepdims=True)
            out = dev_ref[at, 0:1] * (u - jnp.mean(u, axis=-1, keepdims=True) - xhat * slant)
            bias_sum += jnp.sum(out, axis=0, keepdims=True)
            acc_ref[at, :] = out
            first_low[at, :] = out.astype(bf)
            for j, (source, target) in enumerate(((acc_ref, first_hbm), (first_low, low_hbm))):
                store = pltpu.make_async_copy(source.at[at, :], target.at[at, :], out_sem.at[2 * i + j])
                store.start()
                stores.append(store)
        sums_ref[...] = jnp.concatenate([bias_sum, gain_sum, shift_sum, jnp.zeros((5, D), f32)], 0)
        for store in stores:
            store.wait()


def ffn_backward(back_low, slope, wo, wi, low, back, xhat, dev, gain, places, width=512, chunk=512):
    rows = low.shape[0]
    half = wi[0].shape[1]
    cols = pl.BlockSpec((D, width), lambda i: (0, i))
    tall = pl.BlockSpec((width, D), lambda i: (i, 0))
    act = pl.BlockSpec((rows, width), lambda i: (0, i))
    bias = pl.BlockSpec((8, width), lambda i: (0, i))
    full = whole((rows, D))
    return pl.pallas_call(
        lambda *refs: ffn_backward_kernel(*refs, chunk=chunk, places=places),
        out_shape=(shape((D, half), bf),) * 2
        + (shape((8, half), f32),) * 2
        + (shape((rows, D), f32), shape((rows, D), bf), shape((8, D), f32)),
        grid=(half // width,),
        in_specs=[full, act, act, tall, tall, cols, cols, full, anywhere(), anywhere(), whole((rows, 128)), whole((D,))],
        out_specs=[cols] * 2 + [bias] * 2 + [anywhere()] * 2 + [whole((8, D))],
        scratch_shapes=[
            pltpu.VMEM((rows, 2 * width), bf),
            pltpu.VMEM((rows, D), f32),
            pltpu.VMEM((rows, D), f32),
            pltpu.VMEM((rows, D), bf),
            pltpu.SemaphoreType.DMA((2,)),
            pltpu.SemaphoreType.DMA((2 * (rows // chunk),)),
        ],
        name="ffn_backward",
        **settings(40e9, 58),
    )(back_low, *slope, *wo, *wi, low, back, xhat, dev, gain)


def pair_backward(q, k, v, ctx, inv, grad, es):
    size = q.shape[0]
    lane = lax.broadcasted_iota(jnp.int32, (size, 128), 1)
    low = lane < 64
    one = jnp.ones((), bf)
    zero = jnp.zeros((), bf)
    grad = grad * inv
    prod = grad * ctx.astype(f32)
    grad = grad.astype(bf)
    dss = []
    for h in range(2):
        mine = low if h == 0 else ~low
        base = 64 if h == 0 else 0
        delta = -jnp.sum(jnp.where(mine, prod, 0.0), axis=-1, keepdims=True)
        high = delta.astype(bf)
        rest = (delta - high.astype(f32)).astype(bf)
        gh = jnp.where(mine, grad, jnp.where(lane == base, high, jnp.where(lane == base + 1, rest, zero)))
        dp = nt(gh, jnp.where(mine, v, one))
        dss.append((es[h].astype(f32) * dp).astype(bf))
    dq = jnp.where(low, nn(dss[0], k), nn(dss[1], k))
    q_t = q.T
    g_t = grad.T
    dk = jnp.concatenate([nn(q_t[:64], dss[0]), nn(q_t[64:], dss[1])], 0).T
    dv = jnp.concatenate([nn(g_t[:64], es[0]), nn(g_t[64:], es[1])], 0).T
    return dq.astype(bf), dk.astype(bf), dv.astype(bf)


def attention_backward_kernel(
    side_ref, x0, x1, low_ref, qkv_ref, ctx_ref, inv_ref, el_ref, es_ref, wo0, wo1, sums_a, sums_b, sums_c, bias0, bias1,
    out_ref, own_a, own_b, other_a, other_b, small0, small1, grad_ref, *, places_a, places_b,
):
    step = pl.program_id(0)
    half = x0.shape[0]
    rows = 2 * half
    scale = jnp.asarray(0.125, bf)
    low = low_ref[...]
    grad_ref[...] = nt(low, jnp.concatenate([wo0[...], wo1[...]], 0)).astype(bf)
    for first, size, index in slots(rows):
        at = pl.ds(first, size)
        for p in range(2):
            cols = [slice(256 * i + 128 * p, 256 * i + 128 * p + 128) for i in range(3)]
            q = qkv_ref[at, cols[0]] * scale
            k = qkv_ref[at, cols[1]] * scale
            v = qkv_ref[at, cols[2]]
            if size == LONG:
                es = [el_ref[0, 4 * index + 2 * p + h] for h in range(2)]
            else:
                es = [es_ref[0, 4 * (index - half // LONG) + 2 * p + h] for h in range(2)]
            grads = pair_backward(q, k, v, ctx_ref[at, cols[0]], inv_ref[at, cols[0]], grad_ref[at, cols[0]].astype(f32), es)
            for i in range(3):
                out_ref[at, cols[i]] = grads[i]
    packed = out_ref[...]
    wide = (tn(x0[...], packed[:half]) + tn(x1[...], packed[half:])).astype(bf)
    tail = tn(low, ctx_ref[...]).astype(bf)
    for side, (ref_a, ref_b) in enumerate(((own_a, own_b), (other_a, other_b))):
        pieces = [wide[:, 256 * i + 128 * side : 256 * i + 128 * side + 128] for i in range(3)]
        pieces.append(tail[:, 128 * side : 128 * side + 128])
        place_rows(ref_a, jnp.concatenate(pieces[:2], 1), places_a)
        place_rows(ref_b, jnp.concatenate(pieces[2:], 1), places_b)

    @pl.when(step == 0)
    def _():
        for ref, bias in ((small0, bias0), (small1, bias1)):
            ref[0:3, :] = sums_b[1:4, :]
            ref[3:6, :] = sums_c[0:3, :]
            ref[6:8, :] = sums_a[0:2, :]
            ref[8:9, :] = sums_b[0:1, :]
            high = jnp.floor(sums_a[2:3, :] * (1.0 / 256.0))
            ref[9:10, :] = high
            for i in range(bias.shape[1] // D):
                ref[10 + i : 11 + i, :] = bias[0:1, D * i : D * i + D]
            ref[12:16, :] = jnp.zeros((4, D), f32)
            ref[13:14, :] = sums_a[2:3, :] - 256.0 * high

    sums = jnp.sum(packed.astype(f32), axis=0, keepdims=True)
    for side, ref in enumerate((small0, small1)):
        for i in range(2):
            start = pl.multiple_of(i * (D // 2) + 128 * step, 128)
            ref[12:13, pl.ds(start, 128)] = sums[:, 512 * i + 128 * side : 512 * i + 128 * side + 128]


def attention_backward(place, tokens, low, qkv, ctx, inv, e_long, e_short, wo, sums, bias, places_a, places_b):
    half = tokens.shape[0] // 4
    rows = 2 * half
    steps = ctx.shape[1] // 256
    tall = pl.BlockSpec((128, D), lambda i, *_: (i, 0))

    def part(height, width):
        return pl.BlockSpec((height, width), lambda i, *_: (0, i))

    return pl.pallas_call(
        lambda *refs: attention_backward_kernel(*refs, places_a=places_a, places_b=places_b),
        out_shape=(shape((rows, 768 * steps), bf),) + (shape((D, 256 * steps), bf),) * 4 + (shape((16, D), f32),) * 2,
        grid_spec=pltpu.PrefetchScalarGridSpec(
            num_scalar_prefetch=1,
            grid=(steps,),
            in_specs=[
                pl.BlockSpec((half, D), lambda i, side, *_: (side[0], 0)),
                pl.BlockSpec((half, D), lambda i, side, *_: (2 + side[0], 0)),
                whole((rows, D)),
                part(rows, 768),
                part(rows, 256),
                part(rows, 256),
                pl.BlockSpec((1,) + e_long.shape[1:], lambda i, *_: (i, 0, 0, 0)),
                pl.BlockSpec((1,) + e_short.shape[1:], lambda i, *_: (i, 0, 0, 0)),
                tall,
                tall,
            ]
            + [whole((8, D))] * 3
            + [whole(bias[0].shape)] * 2,
            out_specs=[part(rows, 768)] + [part(D, 256)] * 4 + [whole((16, D))] * 2,
            scratch_shapes=[pltpu.VMEM((rows, 256), bf)],
        ),
        name="attention_backward",
        **settings(1e6, 58),
    )(place[0], tokens, tokens, low, qkv, ctx, inv, e_long, e_short, *wo, *sums, *bias)


def tokens_backward_kernel(first_ref, packed_ref, wq0, wq1, wk0, wk1, wv0, wv1, out_ref):
    total = first_ref[...]
    for i in range(packed_ref.shape[1] // 768):
        weights = jnp.concatenate([w[:, 128 * i : 128 * i + 128] for w in (wq0, wq1, wk0, wk1, wv0, wv1)], 1)
        total += nt(packed_ref[:, 768 * i : 768 * i + 768], weights)
    out_ref[...] = total.astype(bf)


def tokens_backward(first, packed, wq, wk, wv):
    rows = first.shape[0]
    chunk = 512
    return pl.pallas_call(
        tokens_backward_kernel,
        out_shape=shape((rows, D), bf),
        grid=(rows // chunk,),
        in_specs=[pl.BlockSpec((chunk, D), lambda i: (i, 0)), pl.BlockSpec((chunk, packed.shape[1]), lambda i: (i, 0))]
        + [whole(wq[0].shape)] * 6,
        out_specs=pl.BlockSpec((chunk, D), lambda i: (i, 0)),
        name="tokens_backward",
        **settings(1e6, 16),
    )(first, packed, *wq, *wk, *wv)


def join_kernel(side_ref, own_ref, other_ref, out_ref, buffer_ref, in_sems, out_sems):
    half = own_ref.shape[0] // 2
    fetches = []
    stores = []
    for i, ref in enumerate((own_ref, other_ref)):
        for j in range(2):
            n = 2 * i + j
            block = 2 * j + (side_ref[0] if i == 0 else 1 - side_ref[0])
            target = out_ref.at[pl.ds(pl.multiple_of(block * half, half), half), :]
            place = buffer_ref.at[n * half : (n + 1) * half, :]
            fetches.append(pltpu.make_async_copy(ref.at[j * half : (j + 1) * half, :], place, in_sems.at[n]))
            stores.append(pltpu.make_async_copy(place, target, out_sems.at[n]))
    for fetch in fetches:
        fetch.start()
    for fetch, store in zip(fetches, stores):
        fetch.wait()
        store.start()
    for store in stores:
        store.wait()


def join_rows(place, own, other):
    return pl.pallas_call(
        join_kernel,
        out_shape=shape((2 * own.shape[0], D), own.dtype),
        grid_spec=pltpu.PrefetchScalarGridSpec(
            num_scalar_prefetch=1,
            grid=(1,),
            in_specs=[anywhere(), anywhere()],
            out_specs=anywhere(),
            scratch_shapes=[
                pltpu.VMEM((2 * own.shape[0], D), own.dtype),
                pltpu.SemaphoreType.DMA((4,)),
                pltpu.SemaphoreType.DMA((4,)),
            ],
        ),
        name="join_rows",
        **settings(1e6, 4),
    )(place[0], own, other)


def exchange_kernel(mine_ref, *refs, chains, small, count, merge, step):
    ins, outs = (refs[:count], refs[count:])
    if small is not None:
        kept, source, first = small
        arrived = ins[source][...] if first is None else ins[source][first : first + 16, :].astype(f32)
        sums = ins[kept][...] + arrived
        sums = sums.astype(bf)
        outs[-1][...] = sums.astype(f32)
    base = 0
    for i, (keep, k0, recv, r0, rows) in enumerate(chains):
        half = rows // 2
        send_ref, keep_ref = (outs[0], outs[1]) if merge else (outs[2 * i], outs[2 * i + 1])
        for ref, side in ((send_ref, 1 - mine_ref[2 * step + i]), (keep_ref, mine_ref[2 * step + i])):
            at = side * half
            mine = ins[keep][pl.ds(pl.multiple_of(k0 + at, 16), half), :].astype(f32)
            sent = ins[recv][pl.ds(pl.multiple_of(r0 + at, 16), half), :].astype(f32)
            ref[base : base + half, :] = (mine + sent).astype(bf)
        end = base + half
        base = end if merge else 0
        if small is not None and i == (len(chains) - 1 if merge else 0):
            send_ref[end : end + 16, :] = sums


def exchange(mine, arrays, chains, small, merge, step):
    columns = arrays[0].shape[1]
    halves = [chain[4] // 2 for chain in chains]
    extra = 0 if small is None else 16
    if merge:
        outs = [shape((sum(halves) + extra, columns), bf), shape((sum(halves), columns), bf)]
    else:
        outs = []
        for i, half in enumerate(halves):
            kind = shape
            outs += [kind((half + (extra if i == 0 else 0), columns), bf), kind((half, columns), bf)]
    if small is not None:
        outs.append(shape((16, D), f32))
    return pl.pallas_call(
        lambda *refs: exchange_kernel(
            *refs, chains=chains, small=small, count=len(arrays), merge=merge, step=step
        ),
        out_shape=tuple(outs),
        grid_spec=pltpu.PrefetchScalarGridSpec(
            num_scalar_prefetch=1,
            grid=(1,),
            in_specs=[whole(v.shape) for v in arrays],
            out_specs=[whole(v.shape) for v in outs],
        ),
        name="exchange",
        **settings(1e6, 8),
    )(mine, *arrays)


def finish_kernel(keep_ref, recv_ref, small_in, *outs):
    rows = keep_ref.shape[0]
    total = keep_ref[...].astype(f32) + recv_ref[0:rows, :].astype(f32)
    for n, ref in enumerate(outs[:4]):
        part = total[(n // 2) * (rows // 2) : (n // 2 + 1) * (rows // 2)]
        for j in range(total.shape[1] // 256):
            ref[:, 128 * j : 128 * j + 128] = part[:, 256 * j + 128 * (n % 2) : 256 * j + 128 * (n % 2) + 128]
    small = small_in[...] + recv_ref[rows : rows + 16, :].astype(f32)
    for n in range(6):
        outs[4 + n][...] = small[n].reshape(D)
    inner_ref, query_ref, value_ref = outs[10:13]
    for i in range(inner_ref.shape[0] // D):
        inner_ref[D * i : D * i + D] = small[10 + i].reshape(D)
    half = query_ref.shape[0]
    query_ref[...] = small[12:13, :half].reshape(half)
    value_ref[...] = small[12:13, half:].reshape(half)
    count = small[9:10, 0:1] * 256.0 + small[13:14, 0:1]
    for n in range(3):
        outs[13 + n][...] = jnp.sqrt(jnp.sum(small[6 + n : 7 + n], axis=1, keepdims=True) / (count * D))


def finish(keep, recv, small, units):
    rows, columns = keep.shape
    half = columns // 2
    outs = [shape((rows // 2, half), f32)] * 4 + [shape((D,), f32)] * 6
    outs += [shape((units,), f32), shape((half,), f32), shape((half,), f32)] + [shape((1, 1), f32)] * 3
    return pl.pallas_call(
        finish_kernel,
        out_shape=tuple(outs),
        grid=(1,),
        in_specs=[whole(v.shape) for v in (keep, recv, small)],
        out_specs=[whole(v.shape) for v in outs],
        name="finish",
        **settings(1e6, 2),
    )(keep, recv, small)


def swap_tensor(value):
    return lax.ppermute(value, "tensor", [(0, 1), (1, 0)])


def dp_bits():
    count = lax.axis_size("dp")
    bits = []
    while (1 << len(bits)) < count:
        bits.append(1 << len(bits))
    return count, bits


def swap_dp(value, bit):
    count, _ = dp_bits()
    return lax.ppermute(value, "dp", [(i, i ^ bit) for i in range(count)])


def after(value, *others):
    return lax.optimization_barrier((value,) + others)[0]


def places_of(order):
    count, bits = dp_bits()
    out = []
    for i in range(count):
        position = 0
        for bit in order:
            position = 2 * position + (i // bit) % 2
        out.append(position)
    return out


def sorted_rows(value, places):
    size = value.shape[0] // len(places)
    source = [places.index(p) for p in range(len(places))]
    return jnp.concatenate([value[i * size : (i + 1) * size] for i in source], 0)


class RowScatter:
    def __init__(self, own, other, order, placed):
        if not placed:
            own, other = [sorted_rows(v, places_of(order)) for v in (own, other)]
        self.pair, self.order = ((own, other), list(order))
        self.split()

    def pick(self, side):
        size = self.pair[0].shape[0] // 2
        a, b = [lax.dynamic_slice_in_dim(v, side * size, size, 0).astype(f32) for v in self.pair]
        return (a + b).astype(bf)

    def resume(self, keep, recv, used):
        self.pair, self.order = ((keep, recv), self.order[used:])
        self.split()

    def split(self):
        mine = (lax.axis_index("dp") // self.order[0]) % 2
        self.send, self.keep = (self.pick(1 - mine), self.pick(mine))

    def step(self, *gates):
        keep = after(self.keep, *gates) if gates else self.keep
        self.pair = (keep, swap_dp(self.send, self.order[0]))
        self.order = self.order[1:]
        if self.order:
            self.split()

    def total(self):
        return self.pair[0].astype(f32) + self.pair[1].astype(f32)

    def ready(self):
        return self.send if self.order else self.pair[1]


def local(
    tokens,
    long_lengths,
    short_lengths,
    query_weight,
    query_bias,
    key_weight,
    value_weight,
    value_bias,
    output_weight,
    output_bias,
    first_gain,
    first_shift,
    inner_weight,
    inner_bias,
    outer_weight_here,
    outer_bias,
    second_gain,
    second_shift,
    out_grad,
):
    count, bits = dp_bits()
    order_a, order_b = (bits, bits[1::-1] + bits[2:])
    order_o = bits
    order_i = bits[:1] + bits[2:3] + bits[1:2] + bits[3:]
    placed = D % (16 * count) == 0
    places_a, places_b, places_o, places_i = [
        places_of(order) if placed else None for order in (order_a, order_b, order_o, order_i)
    ]
    width = query_weight.shape[1]
    place = (lax.axis_index("tensor").reshape(1), long_lengths, short_lengths)
    mine = (lax.axis_index("dp") // jnp.array([v for pair in zip(order_a, order_b) for v in pair], jnp.int32)) % 2
    bq, bv, bi, wq, wk, wv, wo, wi, w2 = [
        (v, swap_tensor(v))
        for v in (
            query_bias,
            value_bias,
            inner_bias,
            query_weight,
            key_weight,
            value_weight,
            output_weight,
            inner_weight,
            outer_weight_here,
        )
    ]
    qkv, ctx, inv, e_long, e_short, xhat, dev, low, sums_a = attention_forward(
        place, tokens, wq, wk, wv, bq, bv, wo, output_bias, first_gain, first_shift
    )
    act, slope0, slope1, block_own, back, back_low, outer_other, sums_b = ffn_forward(
        place, low, wi, bi, w2, xhat, out_grad, first_gain, first_shift, outer_bias, second_gain, second_shift, places_o
    )
    outer_other = swap_tensor(outer_other)
    outer = RowScatter(outer_weight(back_low, act, places_o), outer_other, order_o, placed)
    block_other = swap_tensor(block_own)
    back_low = after(back_low, outer.send, block_other)
    inner_own, inner_other, bias0, bias1, first, first_low, sums_c = ffn_backward(
        back_low, (slope0, slope1), w2, wi, low, back, xhat, dev, first_gain, places_i
    )
    outer.step(sums_c)
    inner_own, inner_other, first_low, first = lax.optimization_barrier(
        (inner_own, inner_other, first_low, first, outer.send)
    )[:4]
    inner = RowScatter(inner_own, swap_tensor(inner_other), order_i, placed)
    first_low = after(first_low, inner.send)
    packed, own_a, own_b, other_a, other_b, small, small_other = attention_backward(
        place, tokens, first_low, qkv, ctx, inv, e_long, e_short, wo, (sums_a, sums_b, sums_c), (bias0, bias1), places_a, places_b
    )
    outer.step(small)
    other_a, other_b, small_other = [swap_tensor(after(v, outer.pair[1])) for v in (other_a, other_b, small_other)]
    inner.step(small)
    own_a, own_b, packed, small, block_own = lax.optimization_barrier(
        (own_a, own_b, packed, small, block_own, outer.pair[1], inner.pair[1])
    )[:5]

    def advance(*gates):
        for chain in (outer, inner):
            if chain.order:
                chain.step(*gates)

    if placed:
        rows = outer.pair[0].shape[0]
        chains = [(0, 0, 1, 0, rows), (2, 0, 3, 0, 2 * rows)]
        send_o, keep_o, send_i, keep_i = exchange(mine, (*outer.pair, *inner.pair), chains, None, False, 2)
        recv_o = swap_dp(send_o, order_o[2])
        own_a = after(own_a, send_o)
        chains = [(0, 0, 1, 0, D), (2, 0, 3, 0, D)]
        send_a, keep_a, send_b, keep_b, small = exchange(mine, (own_a, other_a, own_b, other_b, small, small_other), chains, (4, 5, None), False, 0)
        block_out = join_rows(place, after(block_own, send_a), block_other)
        recv_i = swap_dp(after(send_i, send_a, recv_o), order_i[1])
        outer.resume(after(keep_o, block_out), recv_o, 1)
        packed = after(packed, send_a, block_out, outer.send)
        tokens_own = tokens_backward(first, packed, wq, wk, wv)
        recv_a, recv_b = (swap_dp(send_a, order_a[0]), swap_dp(send_b, order_b[0]))
        keep_a = after(keep_a, tokens_own)
        rows = D // 2
        chains = [(0, 0, 1, 0, rows), (2, 0, 3, 0, rows)]
        send_a, keep_a, send_b, keep_b, small = exchange(mine, (keep_a, recv_a, keep_b, recv_b, small), chains, (4, 1, rows), False, 1)
        tokens_own = after(tokens_own, send_a)
        tokens_other = swap_tensor(tokens_own)
        recv_a, recv_b = (swap_dp(send_a, order_a[1]), swap_dp(send_b, order_b[1]))
        inner.resume(after(keep_i, send_a), recv_i, 1)
        rows = D // 4
        chains = [(0, 0, 1, 0, rows), (2, 0, 3, 0, rows)]
        send, keep, small = exchange(mine, (keep_a, recv_a, keep_b, recv_b, small), chains, (4, 1, rows), True, 2)
        for step in range(2, len(bits) - 1):
            recv = swap_dp(send, order_a[step])
            advance(send)
            rows = keep.shape[0] // 2
            chains = [(0, 0, 1, 0, rows), (0, rows, 1, rows, rows)]
            send, keep, small = exchange(mine, (keep, recv, small), chains, (2, 1, 2 * rows), True, step + 1)
        recv = swap_dp(send, order_a[-1])
        while outer.order or inner.order:
            advance(send)
        tokens_grad = join_rows(place, after(tokens_own, send), tokens_other)
        results = finish(after(keep, tokens_grad), recv, small, inner_bias.shape[0])
        query_grad, key_grad, value_grad, output_grad = results[:4]
        sums = list(results[4:13])
        rms = [v.reshape(()) for v in results[13:]]
    else:
        parts = [RowScatter(own_a, other_a, order_a, placed), RowScatter(own_b, other_b, order_b, placed)]
        small = small + small_other
        tokens_own = tokens_backward(first, packed, wq, wk, wv)
        tokens_grad = join_rows(place, tokens_own, swap_tensor(tokens_own))
        block_out = join_rows(place, block_own, block_other)
        for bit in bits:
            small = small + swap_dp(small, bit)
            for chain in [outer, inner] + parts:
                if chain.order:
                    chain.step()
        part_a, part_b = [part.total().reshape(D // count, -1, 2, 128) for part in parts]
        query_grad, key_grad, value_grad, output_grad = [
            v[:, :, i].reshape(-1, width) for v in (part_a, part_b) for i in range(2)
        ]
        sums = [small[i] for i in range(6)] + [small[10:12].reshape(-1), small[12, :width], small[12, width:]]
        squares = jnp.sum(small[6:9], axis=1)
        rms = jnp.sqrt(squares / ((small[9, 0] * 256.0 + small[13, 0]) * D))
    return (
        block_out,
        tokens_grad,
        query_grad,
        sums[7],
        key_grad,
        value_grad,
        sums[8],
        output_grad.T,
        sums[3],
        sums[4],
        sums[5],
        inner.total(),
        sums[6],
        outer.total().T,
        sums[2],
        sums[0],
        sums[1],
        rms[0],
        rms[1],
        rms[2],
    )


def solution(mesh):
    return jax.shard_map(
        local,
        mesh=mesh,
        in_specs=(
            P("dp", None),
            P("dp"),
            P("dp"),
            P(None, "tensor"),
            P("tensor"),
            P(None, "tensor"),
            P(None, "tensor"),
            P("tensor"),
            P("tensor", None),
            P(),
            P(),
            P(),
            P(None, "tensor"),
            P("tensor"),
            P("tensor", None),
            P(),
            P(),
            P(),
            P("dp", None),
        ),
        out_specs=(
            P("dp", None),
            P("dp", None),
            P("dp", "tensor"),
            P("tensor"),
            P("dp", "tensor"),
            P("dp", "tensor"),
            P("tensor"),
            P("tensor", "dp"),
            P(),
            P(),
            P(),
            P("dp", "tensor"),
            P("tensor"),
            P("tensor", "dp"),
            P(),
            P(),
            P(),
            P(),
            P(),
            P(),
        ),
        check_vma=False,
    )
```

profile of v0, /device:TPU:0, one launch (start us, length us, event | category | flops | bytes accessed | tf_op | source)
XLA Modules:
  0.0 190.1 jit_solution(2661522253275026671)
XLA Ops:
  2.2 3.4 %collective-permute-done.3.bq1 = f32[384]{0:T(512)S(1)} collective-permute-done((f32[384]{0:T(512)}, f32[384]{0:T(512)S(1)}, u32[]{:S(2)}, u32[]{:S(2)}) %collective-permute-start.3) | collective-permute-done | bytes 1568 | tf_op jit(solution)/shard_map/ppermute | solution.py:724
  5.9 1.0 collective-permute-done.4.bv1
  8.9 21.7 %attention_forward.1 = (bf16[1024,2304]{1,0:T(8,128)(2,1)}, bf16[1024,768]{1,0:T(8,128)(2,1)}, f32[1024,768]{1,0:T(8,128)}, bf16[3,4,512,512]{3,2,1,0:T(8,128)(2...) custom-call(s32[1]{0:T(128)} %bitcast.side_ref.refs_0_, ...), custom_call_target="tpu_custom_call" | custom-call | flops 40000000000 | bytes 1000000 | tf_op jit(solution)/shard_map/attention_forward/pallas_call | solution.py:175
  31.1 0.8 copy-done.28
  32.0 25.8 %ffn_forward.1 = (bf16[1024,1536]{1,0:T(8,128)(2,1)}, bf16[1024,1536]{1,0:T(8,128)(2,1)}, bf16[1024,1536]{1,0:T(8,128)(2,1)}, bf16[1024,768]{1,0:T(8,128)(2,1)},...) custom-call(s32[1]{0:T(128)} %bitcast.side_ref.refs_0_, ...), custom_call_target="tpu_custom_call" | custom-call | flops 40000000000 | bytes 1000000 | tf_op jit(solution)/shard_map/ffn_forward/pallas_call | solution.py:313
  58.3 1.9 copy-done.23
  60.2 1.4 copy-done.24
  61.6 3.4 %outer_weight.1 = bf16[768,1536]{1,0:T(8,128)(2,1)S(1)} custom-call(bf16[1024,768]{1,0:T(8,128)(2,1)S(1)} %copy-done.24, bf16[1024,1536]{1,0:T(8,128)(2,1)S(1)} %copy-done.23), custom_call_target="tpu_custom_call" | custom-call | flops 10000000000 | bytes 1000000 | tf_op jit(solution)/shard_map/outer_weight/pallas_call | solution.py:344
  65.0 2.2 %add_convert_fusion.2 = (bf16[384,1536]{1,0:T(8,128)(2,1)S(1)}, bf16[384,1536]{1,0:T(8,128)(2,1)S(1)}) fusion(bf16[768,1536]{1,0:T(8,128)(2,1)} %collective-permute-done.9, s32[]{:T(128)S(6)} %select_n.85, bf16[768,1536]{1,0:T(8,128)(2,1)S(1)} %outer_weight.1, s32[]{:T(128)S(6)} %select_n.84), kind=kLoop, calls=%fused_computation.2 | loop fusion | flops 4718592 | bytes 7077896 | tf_op jit(solution)/shard_map/convert_element_type | solution.py:771
  67.3 2.7 %collective-permute-start.11 = (bf16[384,1536]{1,0:T(8,128)(2,1)S(1)}, bf16[384,1536]{1,0:T(8,128)(2,1)S(1)}, u32[]{:S(2)}, u32[]{:S(2)}) collective-permute-start(bf16[384,1536]{1,0:T(8,128)(2,1)S(1)} %get-tuple-element.217), channel_id=1, source_target_pairs={{0,2},{2,0},{4,6},{6,4},{8,10},{10,8},{12,14},{14,12},{16,18},{18,... | collective-permute-start | bytes 3538952 | tf_op jit(solution)/shard_map/ppermute | solution.py:737
  70.0 26.0 %ffn_backward.1 = (bf16[768,1536]{1,0:T(8,128)(2,1)}, bf16[768,1536]{1,0:T(8,128)(2,1)}, f32[8,1536]{1,0:T(8,128)}, f32[8,1536]{1,0:T(8,128)}, f32[1024,768]{1,0...) custom-call(bf16[1024,768]{1,0:T(8,128)(2,1)} %get-tuple-element.123.refs_0_, ...), custom_call_target="tpu_custom_call" | custom-call | flops 40000000000 | bytes 1000000 | tf_op jit(solution)/shard_map/ffn_backward/pallas_call | solution.py:431
  96.8 1.8 collective-permute-start.13
  98.7 2.9 %collective-permute-done.12 = bf16[768,1536]{1,0:T(8,128)(2,1)S(1)} collective-permute-done((bf16[768,1536]{1,0:T(8,128)(2,1)}, bf16[768,1536]{1,0:T(8,128)(2,1)S(1)}, u32[]{:S(2)}, u32[]{:S(2)}) %collective-permute-start.12) | collective-permute-done | bytes 2359328 | tf_op jit(solution)/shard_map/ppermute | solution.py:724
  102.2 1.8 collective-permute-start.14
  104.0 25.3 %attention_backward.1 = (bf16[1024,2304]{1,0:T(8,128)(2,1)}, bf16[768,768]{1,0:T(8,128)(2,1)}, bf16[768,768]{1,0:T(8,128)(2,1)}, bf16[768,768]{1,0:T(8,128)(2,1)...) custom-call(s32[1]{0:T(128)} %bitcast.side_ref.refs_0_, bf16[2048,768]{1,0:T(8,128)(2,1)} %refs_2_.3, ...), custom_call_target="tpu_custom_call" | custom-call | flops 1000000 | bytes 1000000 | tf_op jit(solution)/shard_map/attention_backward/pallas_call | solution.py:542
  130.3 1.7 exchange.5
  132.0 1.8 collective-permute-start.18
  133.8 1.2 collective-permute-done.17.refs_6_
  135.1 2.0 %exchange.6 = (bf16[400,768]{1,0:T(8,128)(2,1)}, bf16[384,768]{1,0:T(8,128)(2,1)S(1)}, bf16[384,768]{1,0:T(8,128)(2,1)}, bf16[384,768]{1,0:T(8,128)(2,1)S(1)}, f32[16,768]{1,0:T(8,128)S(1)}) custom-call(s32[8]{0:T(128)S(1)} %and_select_fusion.refs_0_, bf16[768,768]{1,0:T(8,128)(2,1)S(1)} %copy-done.5, bf16[768,768]{1,0:T(8,128)(2,1)S(1)} %collective-permute-done.15.refs_2_, ...), custom_call_target="tpu_custom_call" | custom-call | flops 1000000 | bytes 1000000 | tf_op jit(solution)/shard_map/exchange/pallas_call | solution.py:670
  137.1 0.8 copy-done.18
  138.0 0.9 copy-done.20
  138.9 1.5 collective-permute-start.19
  140.3 1.5 collective-permute-start.20
  142.5 1.4 copy-done.2
  143.9 1.4 copy-done.4
  145.3 1.9 %join_rows.2 = bf16[2048,768]{1,0:T(8,128)(2,1)} custom-call(s32[1]{0:T(128)} %bitcast.side_ref.refs_0_, bf16[1024,768]{1,0:T(8,128)(2,1)S(1)} %copy-done.2, bf16[1024,768]{1,0:T(8,128)(2,1)S(1)} %copy-done.4), custom_call_target="tpu_custom_call" | custom-call | flops 1000000 | bytes 1000000 | tf_op jit(solution)/shard_map/join_rows/pallas_call | solution.py:615
  147.2 1.9 add_convert_fusion.8
  149.5 1.1 copy-done.13
  150.6 1.1 copy-done.15
  151.7 4.1 %tokens_backward.1.own_ref = bf16[1024,768]{1,0:T(8,128)(2,1)S(1)} custom-call(f32[1024,768]{1,0:T(8,128)S(1)} %copy-done.1, bf16[1024,2304]{1,0:T(8,128)(2,1)S(1)} %copy-done, bf16[768,384]{1,0:T(8,128)(2,1)S(1)} %copy-done.7, bf16[768,384]{1,0:T(8,128)(2,1)S(1)} %copy-done.11, bf16[768,384]{1,0:T(8,128)(2,1)S(1)} %copy-done.8, ...), custom_call_target="tpu_custom_call" | custom-call | flops 1000000 | bytes 1000000 | tf_op jit(solution)/shard_map/tokens_backward/pallas_call | solution.py:581
  155.8 2.1 %exchange.7 = (bf16[208,768]{1,0:T(8,128)(2,1)S(1)}, bf16[192,768]{1,0:T(8,128)(2,1)S(1)}, bf16[192,768]{1,0:T(8,128)(2,1)S(1)}, bf16[192,768]{1,0:T(8,128)(2,1)S(1)}, f32[16,768]{1,0:T(8,128)S(1)}) custom-call(s32[8]{0:T(128)S(1)} %and_select_fusion.refs_0_, bf16[384,768]{1,0:T(8,128)(2,1)S(1)} %copy-done.19, ...), custom_call_target="tpu_custom_call" | custom-call | flops 1000000 | bytes 1000000 | tf_op jit(solution)/shard_map/exchange/pallas_call | solution.py:670
  157.9 1.6 collective-permute-start.21
  159.5 1.2 collective-permute-start.22
  160.7 1.2 add_convert_fusion.7
  162.4 2.6 %collective-permute-start.29 = (bf16[48,1536]{1,0:T(8,128)(2,1)S(1)}, bf16[48,1536]{1,0:T(8,128)(2,1)S(1)}, u32[]{:S(2)}, u32[]{:S(2)}) collective-permute-start(bf16[48,1536]{1,0:T(8,128)(2,1)S(1)} %get-tuple-element.223), channel_id=1, source_target_pairs={{0,16},{2,18},{4,20},{6,22},{8,24},{10,26},{12,28},{14,30},{16,0},... | collective-permute-start | bytes 442376 | tf_op jit(solution)/shard_map/ppermute | solution.py:737
  165.0 2.1 %collective-permute-done.22.refs_4_ = bf16[192,768]{1,0:T(8,128)(2,1)S(1)} collective-permute-done((bf16[192,768]{1,0:T(8,128)(2,1)S(1)}, bf16[192,768]{1,0:T(8,128)(2,1)S(1)}, u32[]{:S(2)}, u32[]{:S(2)}) %collective-permute-start.22) | collective-permute-done | bytes 294944 | tf_op jit(solution)/shard_map/ppermute | solution.py:737
  167.1 1.0 collective-permute-done.21.refs_2_
  168.1 0.7 exchange.8
  168.8 1.9 collective-permute-start.23
  170.6 2.3 %collective-permute-done.27 = bf16[96,1536]{1,0:T(8,128)(2,1)S(1)} collective-permute-done((bf16[96,1536]{1,0:T(8,128)(2,1)S(1)}, bf16[96,1536]{1,0:T(8,128)(2,1)S(1)}, u32[]{:S(2)}, u32[]{:S(2)}) %collective-permute-start.27) | collective-permute-done | bytes 294944 | tf_op jit(solution)/shard_map/ppermute | solution.py:737
  173.0 2.7 %collective-permute-start.28 = (bf16[48,1536]{1,0:T(8,128)(2,1)S(1)}, bf16[48,1536]{1,0:T(8,128)(2,1)S(1)}, u32[]{:S(2)}, u32[]{:S(2)}) collective-permute-start(bf16[48,1536]{1,0:T(8,128)(2,1)S(1)} %get-tuple-element.225), channel_id=1, source_target_pairs={{0,16},{2,18},{4,20},{6,22},{8,24},{10,26},{12,28},{14,30},{16,0},... | collective-permute-start | bytes 442376 | tf_op jit(solution)/shard_map/ppermute | solution.py:737
  175.6 0.7 add_bitcast_fusion
  176.4 4.4 %collective-permute-done.23.refs_2_ = bf16[208,768]{1,0:T(8,128)(2,1)S(1)} collective-permute-done((bf16[208,768]{1,0:T(8,128)(2,1)S(1)}, bf16[208,768]{1,0:T(8,128)(2,1)S(1)}, u32[]{:S(2)}, u32[]{:S(2)}) %collective-permute-start.23) | collective-permute-done | bytes 319520 | tf_op jit(solution)/shard_map/ppermute | solution.py:737
  180.8 0.6 exchange.9
  181.5 0.7 convert_add_fusion
  182.2 1.9 %join_rows.3 = bf16[2048,768]{1,0:T(8,128)(2,1)} custom-call(s32[1]{0:T(128)} %bitcast.side_ref.refs_0_, bf16[1024,768]{1,0:T(8,128)(2,1)S(1)} %tokens_backward.1.own_ref, bf16[1024,768]{1,0:T(8,128)(2,1)S(1)} %collective-permute-done.24.other_ref), custom_call_target="tpu_custom_call" | custom-call | flops 1000000 | bytes 1000000 | tf_op jit(solution)/shard_map/join_rows/pallas_call | solution.py:615
  184.2 4.9 %collective-permute-done.25.recv_ref = bf16[112,768]{1,0:T(8,128)(2,1)S(1)} collective-permute-done((bf16[112,768]{1,0:T(8,128)(2,1)S(1)}, bf16[112,768]{1,0:T(8,128)(2,1)S(1)}, u32[]{:S(2)}, u32[]{:S(2)}) %collective-permute-start.25) | collective-permute-done | bytes 172064 | tf_op jit(solution)/shard_map/ppermute | solution.py:737
  189.1 0.8 finish.1
  (101 shorter events, 9.1 us)
Async XLA Ops:
  0.7 6.6 %collective-permute-start = (bf16[768,384]{1,0:T(8,128)(2,1)}, bf16[768,384]{1,0:T(8,128)(2,1)S(1)}, u32[]{:S(2)}, u32[]{:S(2)}) collective-permute-start(bf16[768,384]{1,0:T(8,128)(2,1)} %wq0.3), channel_id=1, source_target_pairs={{0,1},{1,0},{2,3},{3,2},{4,5},{5,4},{6,7},{7,6},{8,9},{9,8},{10,11... | collective-permute-start | bytes 1769480 | tf_op jit(solution)/shard_map/ppermute | solution.py:724
  1.2 6.3 %collective-permute-start.1 = (bf16[768,384]{1,0:T(8,128)(2,1)}, bf16[768,384]{1,0:T(8,128)(2,1)S(1)}, u32[]{:S(2)}, u32[]{:S(2)}) collective-permute-start(bf16[768,384]{1,0:T(8,128)(2,1)} %wk0.3), channel_id=1, source_target_pairs={{0,1},{1,0},{2,3},{3,2},{4,5},{5,4},{6,7},{7,6},{8,9},{9,8},{10,11... | collective-permute-start | bytes 1769480 | tf_op jit(solution)/shard_map/ppermute | solution.py:724
  1.3 6.6 %collective-permute-start.2 = (bf16[768,384]{1,0:T(8,128)(2,1)}, bf16[768,384]{1,0:T(8,128)(2,1)S(1)}, u32[]{:S(2)}, u32[]{:S(2)}) collective-permute-start(bf16[768,384]{1,0:T(8,128)(2,1)} %wv0.3), channel_id=1, source_target_pairs={{0,1},{1,0},{2,3},{3,2},{4,5},{5,4},{6,7},{7,6},{8,9},{9,8},{10,11... | collective-permute-start | bytes 1769480 | tf_op jit(solution)/shard_map/ppermute | solution.py:724
  1.7 6.1 %collective-permute-start.5 = (bf16[384,768]{1,0:T(8,128)(2,1)}, bf16[384,768]{1,0:T(8,128)(2,1)S(1)}, u32[]{:S(2)}, u32[]{:S(2)}) collective-permute-start(bf16[384,768]{1,0:T(8,128)(2,1)} %refs_9_.1), channel_id=1, source_target_pairs={{0,1},{1,0},{2,3},{3,2},{4,5},{5,4},{6,7},{7,6},{8,9},{9,8},{10,11... | collective-permute-start | bytes 1769480 | tf_op jit(solution)/shard_map/ppermute | solution.py:724
  1.8 3.8 %collective-permute-start.3 = (f32[384]{0:T(512)}, f32[384]{0:T(512)S(1)}, u32[]{:S(2)}, u32[]{:S(2)}) collective-permute-start(f32[384]{0:T(512)} %bq0.1), channel_id=1, source_target_pairs={{0,1},{1,0},{2,3},{3,2},{4,5},{5,4},{6,7},{7,6},{8,9},{9,8},{10,11... | collective-permute-start | bytes 4616 | tf_op jit(solution)/shard_map/ppermute | solution.py:724
  5.5 2.3 %copy-start.31 = (f32[384]{0:T(512)}, f32[384]{0:T(512)S(1)}, u32[]{:S(2)}) copy-start(f32[384]{0:T(512)S(1)} %collective-permute-done.3.bq1) | copy-start | bytes 4612
  5.6 1.4 collective-permute-start.4
  7.0 23.6 %collective-permute-start.6 = (bf16[768,1536]{1,0:T(8,128)(2,1)}, bf16[768,1536]{1,0:T(8,128)(2,1)S(1)}, u32[]{:S(2)}, u32[]{:S(2)}) collective-permute-start(bf16[768,1536]{1,0:T(8,128)(2,1)} %refs_5_.1), channel_id=1, source_target_pairs={{0,1},{1,0},{2,3},{3,2},{4,5},{5,4},{6,7},{7,6},{8,9},{9,8},{10,11... | collective-permute-start | bytes 7077896 | tf_op jit(solution)/shard_map/ppermute | solution.py:724
  7.3 23.3 %collective-permute-start.8 = (bf16[1536,768]{1,0:T(8,128)(2,1)}, bf16[1536,768]{1,0:T(8,128)(2,1)}, u32[]{:S(2)}, u32[]{:S(2)}) collective-permute-start(bf16[1536,768]{1,0:T(8,128)(2,1)} %refs_3_.1), channel_id=1, source_target_pairs={{0,1},{1,0},{2,3},{3,2},{4,5},{5,4},{6,7},{7,6},{8,9},{9,8},{10,11... | collective-permute-start | bytes 7077896 | tf_op jit(solution)/shard_map/ppermute | solution.py:724
  7.5 23.1 %collective-permute-start.7 = (f32[1536]{0:T(1024)}, f32[1536]{0:T(1024)S(1)}, u32[]{:S(2)}, u32[]{:S(2)}) collective-permute-start(f32[1536]{0:T(1024)} %refs_6_.1), channel_id=1, source_target_pairs={{0,1},{1,0},{2,3},{3,2},{4,5},{5,4},{6,7},{7,6},{8,9},{9,8},{10,11... | collective-permute-start | bytes 18440 | tf_op jit(solution)/shard_map/ppermute | solution.py:724
  57.8 7.3 %collective-permute-start.9 = (bf16[768,1536]{1,0:T(8,128)(2,1)}, bf16[768,1536]{1,0:T(8,128)(2,1)}, u32[]{:S(2)}, u32[]{:S(2)}) collective-permute-start(bf16[768,1536]{1,0:T(8,128)(2,1)} %get-tuple-element.121), channel_id=1, source_target_pairs={{0,1},{1,0},{2,3},{3,2},{4,5},{5,4},{6,7},{7,6},{8,9},{9,8},{10,11... | collective-permute-start | bytes 7077896 | tf_op jit(solution)/shard_map/ppermute | solution.py:724
  58.0 12.0 %collective-permute-start.10 = (bf16[1024,768]{1,0:T(8,128)(2,1)}, bf16[1024,768]{1,0:T(8,128)(2,1)S(1)}, u32[]{:S(2)}, u32[]{:S(2)}) collective-permute-start(bf16[1024,768]{1,0:T(8,128)(2,1)} %get-tuple-element.166.own_ref), channel_id=1, source_target_pairs={{0,1},{1,0},{2,3},{3,2},{4,5},{5,4},{6,7},{7,6},{8,9},{9,8},{10,11... | collective-permute-start | bytes 4718600 | tf_op jit(solution)/shard_map/ppermute | solution.py:724
  67.3 29.2 %collective-permute-start.11 = (bf16[384,1536]{1,0:T(8,128)(2,1)S(1)}, bf16[384,1536]{1,0:T(8,128)(2,1)S(1)}, u32[]{:S(2)}, u32[]{:S(2)}) collective-permute-start(bf16[384,1536]{1,0:T(8,128)(2,1)S(1)} %get-tuple-element.217), channel_id=1, source_target_pairs={{0,2},{2,0},{4,6},{6,4},{8,10},{10,8},{12,14},{14,12},{16,18},{18,... | collective-permute-start | bytes 3538952 | tf_op jit(solution)/shard_map/ppermute | solution.py:737
  70.0 26.0 %copy-start.3 = (bf16[1024,768]{1,0:T(8,128)(2,1)}, bf16[1024,768]{1,0:T(8,128)(2,1)S(1)}, u32[]{:S(2)}) copy-start(bf16[1024,768]{1,0:T(8,128)(2,1)S(1)} %collective-permute-done.10.other_ref) | copy-start | bytes 4718596
  96.0 5.6 %copy-start.25 = (bf16[768,1536]{1,0:T(8,128)(2,1)S(1)}, bf16[768,1536]{1,0:T(8,128)(2,1)}, u32[]{:S(2)}) copy-start(bf16[768,1536]{1,0:T(8,128)(2,1)} %get-tuple-element.135) | copy-start | bytes 7077892
  96.8 4.8 %collective-permute-start.12 = (bf16[768,1536]{1,0:T(8,128)(2,1)}, bf16[768,1536]{1,0:T(8,128)(2,1)S(1)}, u32[]{:S(2)}, u32[]{:S(2)}) collective-permute-start(bf16[768,1536]{1,0:T(8,128)(2,1)} %get-tuple-element.136), channel_id=1, source_target_pairs={{0,1},{1,0},{2,3},{3,2},{4,5},{5,4},{6,7},{7,6},{8,9},{9,8},{10,11... | collective-permute-start | bytes 7077896 | tf_op jit(solution)/shard_map/ppermute | solution.py:724
  96.8 32.5 %collective-permute-start.13 = (bf16[192,1536]{1,0:T(8,128)(2,1)S(1)}, bf16[192,1536]{1,0:T(8,128)(2,1)S(1)}, u32[]{:S(2)}, u32[]{:S(2)}) collective-permute-start(bf16[192,1536]{1,0:T(8,128)(2,1)S(1)} %get-tuple-element.219), channel_id=1, source_target_pairs={{0,4},{2,6},{4,0},{6,2},{8,12},{10,14},{12,8},{14,10},{16,20},{18,... | collective-permute-start | bytes 1769480 | tf_op jit(solution)/shard_map/ppermute | solution.py:737
  102.2 28.1 %collective-permute-start.14 = (bf16[384,1536]{1,0:T(8,128)(2,1)S(1)}, bf16[384,1536]{1,0:T(8,128)(2,1)S(1)}, u32[]{:S(2)}, u32[]{:S(2)}) collective-permute-start(bf16[384,1536]{1,0:T(8,128)(2,1)S(1)} %get-tuple-element.215), channel_id=1, source_target_pairs={{0,2},{2,0},{4,6},{6,4},{8,10},{10,8},{12,14},{14,12},{16,18},{18,... | collective-permute-start | bytes 3538952 | tf_op jit(solution)/shard_map/ppermute | solution.py:737
  104.0 25.9 %copy-start.27 = (s32[8]{0:T(128)S(1)}, s32[8]{0:T(128)}, u32[]{:S(2)}) copy-start(s32[8]{0:T(128)} %constant.98.clone) | copy-start | bytes 100
  129.3 4.5 %copy-start.29 = (f32[16,768]{1,0:T(8,128)S(1)}, f32[16,768]{1,0:T(8,128)}, u32[]{:S(2)}) copy-start(f32[16,768]{1,0:T(8,128)} %get-tuple-element.164) | copy-start | bytes 147460
  129.3 5.8 %copy-start.5 = (bf16[768,768]{1,0:T(8,128)(2,1)S(1)}, bf16[768,768]{1,0:T(8,128)(2,1)}, u32[]{:S(2)}) copy-start(bf16[768,768]{1,0:T(8,128)(2,1)} %get-tuple-element.156.refs_1_) | copy-start | bytes 3538948
  129.3 5.8 %copy-start.6 = (bf16[768,768]{1,0:T(8,128)(2,1)S(1)}, bf16[768,768]{1,0:T(8,128)(2,1)}, u32[]{:S(2)}) copy-start(bf16[768,768]{1,0:T(8,128)(2,1)} %get-tuple-element.159.refs_3_) | copy-start | bytes 3538948
  129.3 5.8 %copy-start.22 = (f32[16,768]{1,0:T(8,128)S(1)}, f32[16,768]{1,0:T(8,128)}, u32[]{:S(2)}) copy-start(f32[16,768]{1,0:T(8,128)} %get-tuple-element.162.refs_5_) | copy-start | bytes 147460
  129.3 5.7 %collective-permute-start.16 = (bf16[768,768]{1,0:T(8,128)(2,1)}, bf16[768,768]{1,0:T(8,128)(2,1)S(1)}, u32[]{:S(2)}, u32[]{:S(2)}) collective-permute-start(bf16[768,768]{1,0:T(8,128)(2,1)} %get-tuple-element.161), channel_id=1, source_target_pairs={{0,1},{1,0},{2,3},{3,2},{4,5},{5,4},{6,7},{7,6},{8,9},{9,8},{10,11... | collective-permute-start | bytes 3538952 | tf_op jit(solution)/shard_map/ppermute | solution.py:724
  129.4 5.6 %collective-permute-start.15 = (bf16[768,768]{1,0:T(8,128)(2,1)}, bf16[768,768]{1,0:T(8,128)(2,1)S(1)}, u32[]{:S(2)}, u32[]{:S(2)}) collective-permute-start(bf16[768,768]{1,0:T(8,128)(2,1)} %get-tuple-element.158), channel_id=1, source_target_pairs={{0,1},{1,0},{2,3},{3,2},{4,5},{5,4},{6,7},{7,6},{8,9},{9,8},{10,11... | collective-permute-start | bytes 3538952 | tf_op jit(solution)/shard_map/ppermute | solution.py:724
  132.0 5.2 %copy-start.16 = (bf16[192,1536]{1,0:T(8,128)(2,1)}, bf16[192,1536]{1,0:T(8,128)(2,1)S(1)}, u32[]{:S(2)}) copy-start(bf16[192,1536]{1,0:T(8,128)(2,1)S(1)} %get-tuple-element.201) | copy-start | bytes 1769476
  132.0 9.9 %collective-permute-start.18 = (bf16[96,1536]{1,0:T(8,128)(2,1)S(1)}, bf16[96,1536]{1,0:T(8,128)(2,1)}, u32[]{:S(2)}, u32[]{:S(2)}) collective-permute-start(bf16[96,1536]{1,0:T(8,128)(2,1)S(1)} %get-tuple-element.155), channel_id=1, source_target_pairs={{0,8},{2,10},{4,12},{6,14},{8,0},{10,2},{12,4},{14,6},{16,24},{18,... | collective-permute-start | bytes 884744 | tf_op jit(solution)/shard_map/ppermute | solution.py:737
  133.8 1.2 collective-permute-start.17
  135.1 14.0 %copy-start.1 = (f32[1024,768]{1,0:T(8,128)S(1)}, f32[1024,768]{1,0:T(8,128)}, u32[]{:S(2)}) copy-start(f32[1024,768]{1,0:T(8,128)} %get-tuple-element.167.first_ref) | copy-start | bytes 9437188
  138.9 16.9 %collective-permute-start.19 = (bf16[400,768]{1,0:T(8,128)(2,1)}, bf16[400,768]{1,0:T(8,128)(2,1)}, u32[]{:S(2)}, u32[]{:S(2)}) collective-permute-start(bf16[400,768]{1,0:T(8,128)(2,1)} %get-tuple-element.165), channel_id=1, source_target_pairs={{0,2},{2,0},{4,6},{6,4},{8,10},{10,8},{12,14},{14,12},{16,18},{18,... | collective-permute-start | bytes 1843208 | tf_op jit(solution)/shard_map/ppermute | solution.py:737
  140.3 15.4 %collective-permute-start.20 = (bf16[384,768]{1,0:T(8,128)(2,1)}, bf16[384,768]{1,0:T(8,128)(2,1)}, u32[]{:S(2)}, u32[]{:S(2)}) collective-permute-start(bf16[384,768]{1,0:T(8,128)(2,1)} %get-tuple-element.175), channel_id=1, source_target_pairs={{0,4},{2,6},{4,0},{6,2},{8,12},{10,14},{12,8},{14,10},{16,20},{18,... | collective-permute-start | bytes 1769480 | tf_op jit(solution)/shard_map/ppermute | solution.py:737
  141.9 18.8 %collective-permute-start.26 = (bf16[192,1536]{1,0:T(8,128)(2,1)}, bf16[192,1536]{1,0:T(8,128)(2,1)}, u32[]{:S(2)}, u32[]{:S(2)}) collective-permute-start(bf16[192,1536]{1,0:T(8,128)(2,1)} %get-tuple-element.203), channel_id=1, source_target_pairs={{0,8},{2,10},{4,12},{6,14},{8,0},{10,2},{12,4},{14,6},{16,24},{18,... | collective-permute-start | bytes 1769480 | tf_op jit(solution)/shard_map/ppermute | solution.py:737
  145.3 3.9 %copy-start = (bf16[1024,2304]{1,0:T(8,128)(2,1)S(1)}, bf16[1024,2304]{1,0:T(8,128)(2,1)}, u32[]{:S(2)}) copy-start(bf16[1024,2304]{1,0:T(8,128)(2,1)} %get-tuple-element.171.packed_ref) | copy-start | bytes 14155780
  145.3 3.9 %copy-start.7 = (bf16[768,384]{1,0:T(8,128)(2,1)S(1)}, bf16[768,384]{1,0:T(8,128)(2,1)}, u32[]{:S(2)}) copy-start(bf16[768,384]{1,0:T(8,128)(2,1)} %wq0.3) | copy-start | bytes 1769476
  145.3 3.9 %copy-start.8 = (bf16[768,384]{1,0:T(8,128)(2,1)S(1)}, bf16[768,384]{1,0:T(8,128)(2,1)}, u32[]{:S(2)}) copy-start(bf16[768,384]{1,0:T(8,128)(2,1)} %wk0.3) | copy-start | bytes 1769476
  145.3 4.1 %copy-start.9 = (bf16[768,384]{1,0:T(8,128)(2,1)S(1)}, bf16[768,384]{1,0:T(8,128)(2,1)}, u32[]{:S(2)}) copy-start(bf16[768,384]{1,0:T(8,128)(2,1)} %wv0.3) | copy-start | bytes 1769476
  145.3 4.3 %copy-start.11 = (bf16[768,384]{1,0:T(8,128)(2,1)S(1)}, bf16[768,384]{1,0:T(8,128)(2,1)}, u32[]{:S(2)}) copy-start(bf16[768,384]{1,0:T(8,128)(2,1)} %copy-done.10) | copy-start | bytes 1769476
  151.7 4.1 %copy-start.19 = (bf16[384,768]{1,0:T(8,128)(2,1)S(1)}, bf16[384,768]{1,0:T(8,128)(2,1)}, u32[]{:S(2)}) copy-start(bf16[384,768]{1,0:T(8,128)(2,1)} %copy-done.18) | copy-start | bytes 1769476
  151.7 4.1 %copy-start.21 = (bf16[384,768]{1,0:T(8,128)(2,1)S(1)}, bf16[384,768]{1,0:T(8,128)(2,1)}, u32[]{:S(2)}) copy-start(bf16[384,768]{1,0:T(8,128)(2,1)} %copy-done.20) | copy-start | bytes 1769476
  155.8 4.9 %copy-start.17 = (bf16[192,1536]{1,0:T(8,128)(2,1)S(1)}, bf16[192,1536]{1,0:T(8,128)(2,1)}, u32[]{:S(2)}) copy-start(bf16[192,1536]{1,0:T(8,128)(2,1)} %copy-done.16) | copy-start | bytes 1769476
  157.9 10.2 %collective-permute-start.21 = (bf16[208,768]{1,0:T(8,128)(2,1)S(1)}, bf16[208,768]{1,0:T(8,128)(2,1)S(1)}, u32[]{:S(2)}, u32[]{:S(2)}) collective-permute-start(bf16[208,768]{1,0:T(8,128)(2,1)S(1)} %get-tuple-element.177), channel_id=1, source_target_pairs={{0,4},{2,6},{4,0},{6,2},{8,12},{10,14},{12,8},{14,10},{16,20},{18,... | collective-permute-start | bytes 958472 | tf_op jit(solution)/shard_map/ppermute | solution.py:737
  159.5 7.6 %collective-permute-start.22 = (bf16[192,768]{1,0:T(8,128)(2,1)S(1)}, bf16[192,768]{1,0:T(8,128)(2,1)S(1)}, u32[]{:S(2)}, u32[]{:S(2)}) collective-permute-start(bf16[192,768]{1,0:T(8,128)(2,1)S(1)} %get-tuple-element.181), channel_id=1, source_target_pairs={{0,2},{2,0},{4,6},{6,4},{8,10},{10,8},{12,14},{14,12},{16,18},{18,... | collective-permute-start | bytes 884744 | tf_op jit(solution)/shard_map/ppermute | solution.py:737
  160.7 21.6 %collective-permute-start.24 = (bf16[1024,768]{1,0:T(8,128)(2,1)S(1)}, bf16[1024,768]{1,0:T(8,128)(2,1)S(1)}, u32[]{:S(2)}, u32[]{:S(2)}) collective-permute-start(bf16[1024,768]{1,0:T(8,128)(2,1)S(1)} %tokens_backward.1.own_ref), channel_id=1, source_target_pairs={{0,1},{1,0},{2,3},{3,2},{4,5},{5,4},{6,7},{7,6},{8,9},{9,8},{10,11... | collective-permute-start | bytes 4718600 | tf_op jit(solution)/shard_map/ppermute | solution.py:724
  161.9 11.0 %collective-permute-start.27 = (bf16[96,1536]{1,0:T(8,128)(2,1)S(1)}, bf16[96,1536]{1,0:T(8,128)(2,1)S(1)}, u32[]{:S(2)}, u32[]{:S(2)}) collective-permute-start(bf16[96,1536]{1,0:T(8,128)(2,1)S(1)} %get-tuple-element.221), channel_id=1, source_target_pairs={{0,4},{2,6},{4,0},{6,2},{8,12},{10,14},{12,8},{14,10},{16,20},{18,... | collective-permute-start | bytes 884744 | tf_op jit(solution)/shard_map/ppermute | solution.py:737
  162.4 13.2 %collective-permute-start.29 = (bf16[48,1536]{1,0:T(8,128)(2,1)S(1)}, bf16[48,1536]{1,0:T(8,128)(2,1)S(1)}, u32[]{:S(2)}, u32[]{:S(2)}) collective-permute-start(bf16[48,1536]{1,0:T(8,128)(2,1)S(1)} %get-tuple-element.223), channel_id=1, source_target_pairs={{0,16},{2,18},{4,20},{6,22},{8,24},{10,26},{12,28},{14,30},{16,0},... | collective-permute-start | bytes 442376 | tf_op jit(solution)/shard_map/ppermute | solution.py:737
  168.8 12.0 %collective-permute-start.23 = (bf16[208,768]{1,0:T(8,128)(2,1)S(1)}, bf16[208,768]{1,0:T(8,128)(2,1)S(1)}, u32[]{:S(2)}, u32[]{:S(2)}) collective-permute-start(bf16[208,768]{1,0:T(8,128)(2,1)S(1)} %get-tuple-element.184), channel_id=1, source_target_pairs={{0,8},{2,10},{4,12},{6,14},{8,0},{10,2},{12,4},{14,6},{16,24},{18,... | collective-permute-start | bytes 958472 | tf_op jit(solution)/shard_map/ppermute | solution.py:737
  173.0 8.5 %collective-permute-start.28 = (bf16[48,1536]{1,0:T(8,128)(2,1)S(1)}, bf16[48,1536]{1,0:T(8,128)(2,1)S(1)}, u32[]{:S(2)}, u32[]{:S(2)}) collective-permute-start(bf16[48,1536]{1,0:T(8,128)(2,1)S(1)} %get-tuple-element.225), channel_id=1, source_target_pairs={{0,16},{2,18},{4,20},{6,22},{8,24},{10,26},{12,28},{14,30},{16,0},... | collective-permute-start | bytes 442376 | tf_op jit(solution)/shard_map/ppermute | solution.py:737
  181.4 7.7 %collective-permute-start.25 = (bf16[112,768]{1,0:T(8,128)(2,1)S(1)}, bf16[112,768]{1,0:T(8,128)(2,1)S(1)}, u32[]{:S(2)}, u32[]{:S(2)}) collective-permute-start(bf16[112,768]{1,0:T(8,128)(2,1)S(1)} %get-tuple-element.186), channel_id=1, source_target_pairs={{0,16},{2,18},{4,20},{6,22},{8,24},{10,26},{12,28},{14,30},{16,0},... | collective-permute-start | bytes 516104 | tf_op jit(solution)/shard_map/ppermute | solution.py:737
  (15 other events, 16.4 us)
where the time goes:
time: 191 us; the launch traced here: 190 us
  Pallas kernels  118 us (62%)
  starting transfers between devices  26.3 us (14%)
  waiting for transfers between devices  23.9 us (13%)
  local copies, waits for them, and re-layouts  12.8 us (7%)
  other arithmetic  7.89 us (4%)
    pallas_call x1, Pallas kernels, ffn_backward(): pl.pallas_call(lambda *refs: ffn_backward_kernel(*refs, chunk=chunk, plac...  26 us
    pallas_call x1, Pallas kernels, ffn_forward(): pl.pallas_call(lambda *refs: ffn_forward_kernel(*refs, chunk=chunk, place...  25.8 us
    pallas_call x1, Pallas kernels, attention_backward(): pl.pallas_call(lambda *refs: attention_backward_kernel(*refs, places_a=pl...  25.3 us
    ppermute x14, starting transfers between devices, swap_dp(): return lax.ppermute(value, 'dp', [(i, i ^ bit) for i in range(count)])  22.3 us
    pallas_call x1, Pallas kernels, attention_forward(): pl.pallas_call(attention_forward_kernel, out_shape=(shape((rows, steps *...  21.7 us
    ppermute x14, waiting for transfers between devices, swap_dp(): return lax.ppermute(value, 'dp', [(i, i ^ bit) for i in range(count)])  15.4 us
    unnamed x66, local copies, waits for them, and re-layouts  12.8 us
    ppermute x16, waiting for transfers between devices, swap_tensor(): return lax.ppermute(value, 'tensor', [(0, 1), (1, 0)])  8.54 us
  transfers between devices with their start and end apart: 30, of which 11 were waited for; matrix products, arithmetic and copies ran while one was open for 4% of the time, Pallas kernels for 48%

commit v1 on v0

--- a/solution.py
+++ b/solution.py
@@ -98,7 +98,7 @@
 
 def attention_forward_kernel(
     side_ref, long_ref, short_ref,
-    x0, x1, wq0, wq1, wk0, wk1, wv0, wv1, bq0, bq1, bv0, bv1, wo0, wo1, bo_ref, gain_ref, shift_ref,
+    x0, x1, wq0, wq1, wk0, wk1, wv0, wv1, bias0, bias1, wo0, wo1, bo_ref, gain_ref, shift_ref,
     qkv_ref, ctx_ref, inv_ref, el_ref, es_ref, xhat_ref, dev_ref, low_ref, sums_ref, acc_ref, all_ref,
 ):
     step = pl.program_id(0)
@@ -107,7 +107,8 @@
     zero = jnp.zeros((1, 256), f32)
     cols = pl.ds(pl.multiple_of(128 * step, 128), 128)
     weights = jnp.concatenate([w[...] for w in (wq0, wq1, wk0, wk1, wv0, wv1)], 1)
-    bias = [b[cols].reshape(1, 128) for b in (bq0, bq1, bv0, bv1)]
+    late = pl.ds(pl.multiple_of(wo0.shape[0] + 128 * step, 128), 128)
+    bias = [b[at].reshape(1, 128) for at in (cols, late) for b in (bias0, bias1)]
     bias = jnp.concatenate(bias[:2] + [zero] + bias[2:], 1)
     for i, x in enumerate((x0, x1)):
         qkv_ref[i * half : (i + 1) * half, :] = (nn(x[...], weights) + bias).astype(bf)
@@ -160,7 +161,7 @@
         sums_ref[...] = jnp.concatenate([resid, attn, count, jnp.zeros((5, D), f32)], 0)
 
 
-def attention_forward(place, tokens, wq, wk, wv, bq, bv, wo, bo, gain, shift):
+def attention_forward(place, tokens, wq, wk, wv, bias, wo, bo, gain, shift):
     half = tokens.shape[0] // 4
     rows = 2 * half
     width = wq[0].shape[1]
@@ -193,7 +194,7 @@
                 pl.BlockSpec((half, D), lambda i, side, *_: (2 + side[0], 0)),
             ]
             + [wide] * 6
-            + [whole((width,))] * 4
+            + [whole(bias[0].shape)] * 2
             + [whole((width, D))] * 2
             + [whole((D,))] * 3,
             out_specs=[
@@ -211,7 +212,7 @@
         ),
         name="attention_forward",
         **settings(40e9, 58),
-    )(*place, tokens, tokens, *wq, *wk, *wv, *bq, *bv, *wo, bo, gain, shift)
+    )(*place, tokens, tokens, *wq, *wk, *wv, *bias, *wo, bo, gain, shift)
 
 
 def gelu_parts(v):
@@ -240,8 +241,9 @@
             fetch.start()
 
     cols = pl.ds(pl.multiple_of(width * step, width), width)
+    place = pl.ds(pl.multiple_of(bi0.shape[0] - act1.shape[1] + width * step, 128), width)
     win = jnp.concatenate([wi0[...], wi1[...]], 1)
-    bias = jnp.concatenate([b[cols].reshape(1, width) for b in (bi0, bi1)], 1)
+    bias = jnp.concatenate([b[place].reshape(1, width) for b in (bi0, bi1)], 1)
     wout = jnp.concatenate([wo0[...], wo1[...]], 0)
     for first in range(0, rows, chunk):
         at = pl.ds(first, chunk)
@@ -317,7 +319,7 @@
         grid_spec=pltpu.PrefetchScalarGridSpec(
             num_scalar_prefetch=3,
             grid=(half // width,),
-            in_specs=[whole((rows, D)), cols, cols, whole((half,)), whole((half,)), tall, tall, anywhere(), anywhere()] + [row] * 5,
+            in_specs=[whole((rows, D)), cols, cols, whole(bi[0].shape), whole(bi[1].shape), tall, tall, anywhere(), anywhere()] + [row] * 5,
             out_specs=[act] * 3 + [anywhere()] * 3 + [whole((D, half)), whole((8, D))],
             scratch_shapes=[
                 pltpu.VMEM((rows, D), f32),
@@ -824,12 +826,10 @@
     width = query_weight.shape[1]
     place = (lax.axis_index("tensor").reshape(1), long_lengths, short_lengths)
     mine = (lax.axis_index("dp") // jnp.array([v for pair in zip(order_a, order_b) for v in pair], jnp.int32)) % 2
-    bq, bv, bi, wq, wk, wv, wo, wi, w2 = [
+    bias, wq, wk, wv, wo, wi, w2 = [
         (v, swap_tensor(v))
         for v in (
-            query_bias,
-            value_bias,
-            inner_bias,
+            jnp.concatenate([query_bias, value_bias, inner_bias]),
             query_weight,
             key_weight,
             value_weight,
@@ -839,10 +839,10 @@
         )
     ]
     qkv, ctx, inv, e_long, e_short, xhat, dev, low, sums_a = attention_forward(
-        place, tokens, wq, wk, wv, bq, bv, wo, output_bias, first_gain, first_shift
+        place, tokens, wq, wk, wv, bias, wo, output_bias, first_gain, first_shift
     )
     act, slope0, slope1, block_own, back, back_low, outer_other, sums_b = ffn_forward(
-        place, low, wi, bi, w2, xhat, out_grad, first_gain, first_shift, outer_bias, second_gain, second_shift, places_o
+        place, low, wi, bias, w2, xhat, out_grad, first_gain, first_shift, outer_bias, second_gain, second_shift, places_o
     )
     outer_other = swap_tensor(outer_other)
     outer = RowScatter(outer_weight(back_low, act, places_o), outer_other, order_o, placed)

time: 191 us -> 189 us (0.990)
  waiting for transfers between devices: 23.9 us -> 20.2 us
  local copies, waits for them, and re-layouts: 12.8 us -> 15.1 us
    ppermute x16 -> x14, waiting for transfers between devices: 8.54 us -> 5.24 us  [swap_tensor(): return lax.ppermute(value, 'tensor', [(0, 1), (1, 0)])]
    ppermute x16 -> x14, starting transfers between devices: 3.97 us -> 3.27 us  [swap_tensor(): return lax.ppermute(value, 'tensor', [(0, 1), (1, 0)])]
  transfers between devices with their start and end apart: 30 -> 28, of which waited for: 11 -> 10; matrix products, arithmetic and copies ran while one was open for 4% -> 5% of each run, Pallas kernels for 48% -> 49%
where the time goes in v1:
time: 189 us; the launch traced here: 188 us
  Pallas kernels  118 us (62%)
  starting transfers between devices  25.7 us (14%)
  waiting for transfers between devices  20.2 us (11%)
  local copies, waits for them, and re-layouts  15.1 us (8%)
  other arithmetic  7.89 us (4%)
    pallas_call x1, Pallas kernels, ffn_backward(): pl.pallas_call(lambda *refs: ffn_backward_kernel(*refs, chunk=chunk, plac...  26 us
    pallas_call x1, Pallas kernels, ffn_forward(): pl.pallas_call(lambda *refs: ffn_forward_kernel(*refs, chunk=chunk, place...  25.8 us
    pallas_call x1, Pallas kernels, attention_backward(): pl.pallas_call(lambda *refs: attention_backward_kernel(*refs, places_a=pl...  25.3 us
    ppermute x14, starting transfers between devices, swap_dp(): return lax.ppermute(value, 'dp', [(i, i ^ bit) for i in range(count)])  22.5 us
    pallas_call x1, Pallas kernels, attention_forward(): pl.pallas_call(attention_forward_kernel, out_shape=(shape((rows, steps *...  21.6 us
    ppermute x14, waiting for transfers between devices, swap_dp(): return lax.ppermute(value, 'dp', [(i, i ^ bit) for i in range(count)])  15 us
    unnamed x66, local copies, waits for them, and re-layouts  14.4 us
    pallas_call x5, Pallas kernels, exchange(): pl.pallas_call(lambda *refs: exchange_kernel(*refs, chains=chains, small=...  7.12 us
  transfers between devices with their start and end apart: 28, of which 10 were waited for; matrix products, arithmetic and copies ran while one was open for 5% of the time, Pallas kernels for 49%

profile of v1, /device:TPU:0, one launch (start us, length us, event | category | flops | bytes accessed | tf_op | source)
XLA Modules:
  0.0 188.1 jit_solution(18041093766161691411)
XLA Ops:
  1.8 0.7 constant_dynamic-update-slice_fusion.2
  2.5 0.7 constant_dynamic-update-slice_fusion.1
  3.1 0.7 constant_dynamic-update-slice_fusion.bias0.refs_6_
  4.3 1.1 collective-permute-done.3.bias1.refs_7_
  7.1 21.6 %attention_forward.1 = (bf16[1024,2304]{1,0:T(8,128)(2,1)}, bf16[1024,768]{1,0:T(8,128)(2,1)}, f32[1024,768]{1,0:T(8,128)}, bf16[3,4,512,512]{3,2,1,0:T(8,128)(2...) custom-call(s32[1]{0:T(128)} %bitcast.side_ref.refs_0_, ...), custom_call_target="tpu_custom_call" | custom-call | flops 40000000000 | bytes 1000000 | tf_op jit(solution)/shard_map/attention_forward/pallas_call | solution.py:176
  28.8 1.4 copy-done.28
  30.1 25.8 %ffn_forward.1 = (bf16[1024,1536]{1,0:T(8,128)(2,1)}, bf16[1024,1536]{1,0:T(8,128)(2,1)}, bf16[1024,1536]{1,0:T(8,128)(2,1)}, bf16[1024,768]{1,0:T(8,128)(2,1)},...) custom-call(s32[1]{0:T(128)} %bitcast.side_ref.refs_0_, ...), custom_call_target="tpu_custom_call" | custom-call | flops 40000000000 | bytes 1000000 | tf_op jit(solution)/shard_map/ffn_forward/pallas_call | solution.py:315
  56.5 1.9 %copy-done.23 = bf16[1024,1536]{1,0:T(8,128)(2,1)S(1)} copy-done((bf16[1024,1536]{1,0:T(8,128)(2,1)S(1)}, bf16[1024,1536]{1,0:T(8,128)(2,1)}, u32[]{:S(2)}) %copy-start.23) | copy-done | bytes 3145752
  58.4 1.4 copy-done.24
  59.8 3.4 %outer_weight.1 = bf16[768,1536]{1,0:T(8,128)(2,1)S(1)} custom-call(bf16[1024,768]{1,0:T(8,128)(2,1)S(1)} %copy-done.24, bf16[1024,1536]{1,0:T(8,128)(2,1)S(1)} %copy-done.23), custom_call_target="tpu_custom_call" | custom-call | flops 10000000000 | bytes 1000000 | tf_op jit(solution)/shard_map/outer_weight/pallas_call | solution.py:346
  63.2 2.2 %add_convert_fusion.2 = (bf16[384,1536]{1,0:T(8,128)(2,1)S(1)}, bf16[384,1536]{1,0:T(8,128)(2,1)S(1)}) fusion(bf16[768,1536]{1,0:T(8,128)(2,1)} %collective-permute-done.7, s32[]{:T(128)S(6)} %select_n.85, bf16[768,1536]{1,0:T(8,128)(2,1)S(1)} %outer_weight.1, s32[]{:T(128)S(6)} %select_n.84), kind=kLoop, calls=%fused_computation.2 | loop fusion | flops 4718592 | bytes 7077896 | tf_op jit(solution)/shard_map/convert_element_type | solution.py:773
  65.5 2.9 %collective-permute-start.9 = (bf16[384,1536]{1,0:T(8,128)(2,1)S(1)}, bf16[384,1536]{1,0:T(8,128)(2,1)S(1)}, u32[]{:S(2)}, u32[]{:S(2)}) collective-permute-start(bf16[384,1536]{1,0:T(8,128)(2,1)S(1)} %get-tuple-element.217), channel_id=1, source_target_pairs={{0,2},{2,0},{4,6},{6,4},{8,10},{10,8},{12,14},{14,12},{16,18},{18,... | collective-permute-start | bytes 3538952 | tf_op jit(solution)/shard_map/ppermute | solution.py:739
  68.3 26.0 %ffn_backward.1 = (bf16[768,1536]{1,0:T(8,128)(2,1)}, bf16[768,1536]{1,0:T(8,128)(2,1)}, f32[8,1536]{1,0:T(8,128)}, f32[8,1536]{1,0:T(8,128)}, f32[1024,768]{1,0...) custom-call(bf16[1024,768]{1,0:T(8,128)(2,1)} %get-tuple-element.123.refs_0_, ...), custom_call_target="tpu_custom_call" | custom-call | flops 40000000000 | bytes 1000000 | tf_op jit(solution)/shard_map/ffn_backward/pallas_call | solution.py:433
  95.0 1.8 collective-permute-start.11
  96.8 2.9 %collective-permute-done.10 = bf16[768,1536]{1,0:T(8,128)(2,1)S(1)} collective-permute-done((bf16[768,1536]{1,0:T(8,128)(2,1)}, bf16[768,1536]{1,0:T(8,128)(2,1)S(1)}, u32[]{:S(2)}, u32[]{:S(2)}) %collective-permute-start.10) | collective-permute-done | bytes 2359328 | tf_op jit(solution)/shard_map/ppermute | solution.py:726
  100.4 1.8 collective-permute-start.12
  102.2 25.3 %attention_backward.1 = (bf16[1024,2304]{1,0:T(8,128)(2,1)}, bf16[768,768]{1,0:T(8,128)(2,1)}, bf16[768,768]{1,0:T(8,128)(2,1)}, bf16[768,768]{1,0:T(8,128)(2,1)...) custom-call(s32[1]{0:T(128)} %bitcast.side_ref.refs_0_, bf16[2048,768]{1,0:T(8,128)(2,1)} %refs_2_.3, ...), custom_call_target="tpu_custom_call" | custom-call | flops 1000000 | bytes 1000000 | tf_op jit(solution)/shard_map/attention_backward/pallas_call | solution.py:544
  128.4 1.7 exchange.5
  130.1 1.8 collective-permute-start.16
  132.0 1.2 collective-permute-done.15.refs_6_
  133.2 2.0 %exchange.6 = (bf16[400,768]{1,0:T(8,128)(2,1)}, bf16[384,768]{1,0:T(8,128)(2,1)S(1)}, bf16[384,768]{1,0:T(8,128)(2,1)}, bf16[384,768]{1,0:T(8,128)(2,1)S(1)}, f32[16,768]{1,0:T(8,128)S(1)}) custom-call(s32[8]{0:T(128)S(1)} %and_select_fusion.refs_0_, bf16[768,768]{1,0:T(8,128)(2,1)S(1)} %copy-done.5, bf16[768,768]{1,0:T(8,128)(2,1)S(1)} %collective-permute-done.13.refs_2_, ...), custom_call_target="tpu_custom_call" | custom-call | flops 1000000 | bytes 1000000 | tf_op jit(solution)/shard_map/exchange/pallas_call | solution.py:672
  135.3 0.8 copy-done.18
  136.1 0.9 copy-done.20
  137.0 1.5 collective-permute-start.17
  138.5 1.5 collective-permute-start.18
  140.7 1.4 copy-done.2
  142.1 1.4 copy-done.4
  143.5 1.9 %join_rows.2 = bf16[2048,768]{1,0:T(8,128)(2,1)} custom-call(s32[1]{0:T(128)} %bitcast.side_ref.refs_0_, bf16[1024,768]{1,0:T(8,128)(2,1)S(1)} %copy-done.2, bf16[1024,768]{1,0:T(8,128)(2,1)S(1)} %copy-done.4), custom_call_target="tpu_custom_call" | custom-call | flops 1000000 | bytes 1000000 | tf_op jit(solution)/shard_map/join_rows/pallas_call | solution.py:617
  145.5 1.9 add_convert_fusion.8
  147.8 1.1 copy-done.13
  148.8 1.1 copy-done.15
  149.9 4.1 %tokens_backward.1.own_ref = bf16[1024,768]{1,0:T(8,128)(2,1)S(1)} custom-call(f32[1024,768]{1,0:T(8,128)S(1)} %copy-done.1, bf16[1024,2304]{1,0:T(8,128)(2,1)S(1)} %copy-done, bf16[768,384]{1,0:T(8,128)(2,1)S(1)} %copy-done.7, bf16[768,384]{1,0:T(8,128)(2,1)S(1)} %copy-done.11, bf16[768,384]{1,0:T(8,128)(2,1)S(1)} %copy-done.8, ...), custom_call_target="tpu_custom_call" | custom-call | flops 1000000 | bytes 1000000 | tf_op jit(solution)/shard_map/tokens_backward/pallas_call | solution.py:583
  154.0 2.1 %exchange.7 = (bf16[208,768]{1,0:T(8,128)(2,1)S(1)}, bf16[192,768]{1,0:T(8,128)(2,1)S(1)}, bf16[192,768]{1,0:T(8,128)(2,1)S(1)}, bf16[192,768]{1,0:T(8,128)(2,1)S(1)}, f32[16,768]{1,0:T(8,128)S(1)}) custom-call(s32[8]{0:T(128)S(1)} %and_select_fusion.refs_0_, bf16[384,768]{1,0:T(8,128)(2,1)S(1)} %copy-done.19, ...), custom_call_target="tpu_custom_call" | custom-call | flops 1000000 | bytes 1000000 | tf_op jit(solution)/shard_map/exchange/pallas_call | solution.py:672
  156.1 1.6 collective-permute-start.19
  157.7 1.1 collective-permute-start.20
  158.8 1.2 add_convert_fusion.7
  160.6 2.6 %collective-permute-start.27 = (bf16[48,1536]{1,0:T(8,128)(2,1)S(1)}, bf16[48,1536]{1,0:T(8,128)(2,1)S(1)}, u32[]{:S(2)}, u32[]{:S(2)}) collective-permute-start(bf16[48,1536]{1,0:T(8,128)(2,1)S(1)} %get-tuple-element.223), channel_id=1, source_target_pairs={{0,16},{2,18},{4,20},{6,22},{8,24},{10,26},{12,28},{14,30},{16,0},... | collective-permute-start | bytes 442376 | tf_op jit(solution)/shard_map/ppermute | solution.py:739
  163.2 2.0 %collective-permute-done.20.refs_4_ = bf16[192,768]{1,0:T(8,128)(2,1)S(1)} collective-permute-done((bf16[192,768]{1,0:T(8,128)(2,1)S(1)}, bf16[192,768]{1,0:T(8,128)(2,1)S(1)}, u32[]{:S(2)}, u32[]{:S(2)}) %collective-permute-start.20) | collective-permute-done | bytes 294944 | tf_op jit(solution)/shard_map/ppermute | solution.py:739
  165.2 0.9 collective-permute-done.19.refs_2_
  166.9 1.9 %collective-permute-start.21 = (bf16[208,768]{1,0:T(8,128)(2,1)S(1)}, bf16[208,768]{1,0:T(8,128)(2,1)S(1)}, u32[]{:S(2)}, u32[]{:S(2)}) collective-permute-start(bf16[208,768]{1,0:T(8,128)(2,1)S(1)} %get-tuple-element.184), channel_id=1, source_target_pairs={{0,8},{2,10},{4,12},{6,14},{8,0},{10,2},{12,4},{14,6},{16,24},{18,... | collective-permute-start | bytes 958472 | tf_op jit(solution)/shard_map/ppermute | solution.py:739
  168.7 2.3 %collective-permute-done.25 = bf16[96,1536]{1,0:T(8,128)(2,1)S(1)} collective-permute-done((bf16[96,1536]{1,0:T(8,128)(2,1)S(1)}, bf16[96,1536]{1,0:T(8,128)(2,1)S(1)}, u32[]{:S(2)}, u32[]{:S(2)}) %collective-permute-start.25) | collective-permute-done | bytes 294944 | tf_op jit(solution)/shard_map/ppermute | solution.py:739
  171.1 2.7 %collective-permute-start.26 = (bf16[48,1536]{1,0:T(8,128)(2,1)S(1)}, bf16[48,1536]{1,0:T(8,128)(2,1)S(1)}, u32[]{:S(2)}, u32[]{:S(2)}) collective-permute-start(bf16[48,1536]{1,0:T(8,128)(2,1)S(1)} %get-tuple-element.225), channel_id=1, source_target_pairs={{0,16},{2,18},{4,20},{6,22},{8,24},{10,26},{12,28},{14,30},{16,0},... | collective-permute-start | bytes 442376 | tf_op jit(solution)/shard_map/ppermute | solution.py:739
  173.7 0.7 add_bitcast_fusion
  174.5 4.4 %collective-permute-done.21.refs_2_ = bf16[208,768]{1,0:T(8,128)(2,1)S(1)} collective-permute-done((bf16[208,768]{1,0:T(8,128)(2,1)S(1)}, bf16[208,768]{1,0:T(8,128)(2,1)S(1)}, u32[]{:S(2)}, u32[]{:S(2)}) %collective-permute-start.21) | collective-permute-done | bytes 319520 | tf_op jit(solution)/shard_map/ppermute | solution.py:739
  179.6 0.7 convert_add_fusion
  180.4 1.9 %join_rows.3 = bf16[2048,768]{1,0:T(8,128)(2,1)} custom-call(s32[1]{0:T(128)} %bitcast.side_ref.refs_0_, bf16[1024,768]{1,0:T(8,128)(2,1)S(1)} %tokens_backward.1.own_ref, bf16[1024,768]{1,0:T(8,128)(2,1)S(1)} %collective-permute-done.22.other_ref), custom_call_target="tpu_custom_call" | custom-call | flops 1000000 | bytes 1000000 | tf_op jit(solution)/shard_map/join_rows/pallas_call | solution.py:617
  182.3 4.8 %collective-permute-done.23.recv_ref = bf16[112,768]{1,0:T(8,128)(2,1)S(1)} collective-permute-done((bf16[112,768]{1,0:T(8,128)(2,1)S(1)}, bf16[112,768]{1,0:T(8,128)(2,1)S(1)}, u32[]{:S(2)}, u32[]{:S(2)}) %collective-permute-start.23) | collective-permute-done | bytes 172064 | tf_op jit(solution)/shard_map/ppermute | solution.py:739
  187.1 0.8 finish.1
  (99 shorter events, 9.2 us)
Async XLA Ops:
  0.7 5.1 %collective-permute-start = (bf16[768,384]{1,0:T(8,128)(2,1)}, bf16[768,384]{1,0:T(8,128)(2,1)S(1)}, u32[]{:S(2)}, u32[]{:S(2)}) collective-permute-start(bf16[768,384]{1,0:T(8,128)(2,1)} %wq0.3), channel_id=1, source_target_pairs={{0,1},{1,0},{2,3},{3,2},{4,5},{5,4},{6,7},{7,6},{8,9},{9,8},{10,11... | collective-permute-start | bytes 1769480 | tf_op jit(solution)/shard_map/ppermute | solution.py:726
  1.2 4.7 %collective-permute-start.1 = (bf16[768,384]{1,0:T(8,128)(2,1)}, bf16[768,384]{1,0:T(8,128)(2,1)S(1)}, u32[]{:S(2)}, u32[]{:S(2)}) collective-permute-start(bf16[768,384]{1,0:T(8,128)(2,1)} %wk0.3), channel_id=1, source_target_pairs={{0,1},{1,0},{2,3},{3,2},{4,5},{5,4},{6,7},{7,6},{8,9},{9,8},{10,11... | collective-permute-start | bytes 1769480 | tf_op jit(solution)/shard_map/ppermute | solution.py:726
  1.3 4.6 %collective-permute-start.2 = (bf16[768,384]{1,0:T(8,128)(2,1)}, bf16[768,384]{1,0:T(8,128)(2,1)S(1)}, u32[]{:S(2)}, u32[]{:S(2)}) collective-permute-start(bf16[768,384]{1,0:T(8,128)(2,1)} %wv0.3), channel_id=1, source_target_pairs={{0,1},{1,0},{2,3},{3,2},{4,5},{5,4},{6,7},{7,6},{8,9},{9,8},{10,11... | collective-permute-start | bytes 1769480 | tf_op jit(solution)/shard_map/ppermute | solution.py:726
  1.7 4.2 %collective-permute-start.4 = (bf16[384,768]{1,0:T(8,128)(2,1)}, bf16[384,768]{1,0:T(8,128)(2,1)S(1)}, u32[]{:S(2)}, u32[]{:S(2)}) collective-permute-start(bf16[384,768]{1,0:T(8,128)(2,1)} %refs_9_.1), channel_id=1, source_target_pairs={{0,1},{1,0},{2,3},{3,2},{4,5},{5,4},{6,7},{7,6},{8,9},{9,8},{10,11... | collective-permute-start | bytes 1769480 | tf_op jit(solution)/shard_map/ppermute | solution.py:726
  3.8 2.1 %copy-start.31 = (f32[2304]{0:T(1024)}, f32[2304]{0:T(1024)S(1)}, u32[]{:S(2)}) copy-start(f32[2304]{0:T(1024)S(1)} %constant_dynamic-update-slice_fusion.bias0.refs_6_) | copy-start | bytes 27652
  3.8 1.5 collective-permute-start.3
  5.4 23.4 %collective-permute-start.5 = (bf16[768,1536]{1,0:T(8,128)(2,1)}, bf16[768,1536]{1,0:T(8,128)(2,1)S(1)}, u32[]{:S(2)}, u32[]{:S(2)}) collective-permute-start(bf16[768,1536]{1,0:T(8,128)(2,1)} %refs_5_.1), channel_id=1, source_target_pairs={{0,1},{1,0},{2,3},{3,2},{4,5},{5,4},{6,7},{7,6},{8,9},{9,8},{10,11... | collective-permute-start | bytes 7077896 | tf_op jit(solution)/shard_map/ppermute | solution.py:726
  5.7 23.0 %collective-permute-start.6 = (bf16[1536,768]{1,0:T(8,128)(2,1)}, bf16[1536,768]{1,0:T(8,128)(2,1)}, u32[]{:S(2)}, u32[]{:S(2)}) collective-permute-start(bf16[1536,768]{1,0:T(8,128)(2,1)} %refs_3_.1), channel_id=1, source_target_pairs={{0,1},{1,0},{2,3},{3,2},{4,5},{5,4},{6,7},{7,6},{8,9},{9,8},{10,11... | collective-permute-start | bytes 7077896 | tf_op jit(solution)/shard_map/ppermute | solution.py:726
  55.9 7.3 %collective-permute-start.7 = (bf16[768,1536]{1,0:T(8,128)(2,1)}, bf16[768,1536]{1,0:T(8,128)(2,1)}, u32[]{:S(2)}, u32[]{:S(2)}) collective-permute-start(bf16[768,1536]{1,0:T(8,128)(2,1)} %get-tuple-element.121), channel_id=1, source_target_pairs={{0,1},{1,0},{2,3},{3,2},{4,5},{5,4},{6,7},{7,6},{8,9},{9,8},{10,11... | collective-permute-start | bytes 7077896 | tf_op jit(solution)/shard_map/ppermute | solution.py:726
  56.3 12.0 %collective-permute-start.8 = (bf16[1024,768]{1,0:T(8,128)(2,1)}, bf16[1024,768]{1,0:T(8,128)(2,1)S(1)}, u32[]{:S(2)}, u32[]{:S(2)}) collective-permute-start(bf16[1024,768]{1,0:T(8,128)(2,1)} %get-tuple-element.166.own_ref), channel_id=1, source_target_pairs={{0,1},{1,0},{2,3},{3,2},{4,5},{5,4},{6,7},{7,6},{8,9},{9,8},{10,11... | collective-permute-start | bytes 4718600 | tf_op jit(solution)/shard_map/ppermute | solution.py:726
  56.5 1.9 %copy-start.23 = (bf16[1024,1536]{1,0:T(8,128)(2,1)S(1)}, bf16[1024,1536]{1,0:T(8,128)(2,1)}, u32[]{:S(2)}) copy-start(bf16[1024,1536]{1,0:T(8,128)(2,1)} %get-tuple-element.120.refs_1_) | copy-start | bytes 9437188
  65.5 29.2 %collective-permute-start.9 = (bf16[384,1536]{1,0:T(8,128)(2,1)S(1)}, bf16[384,1536]{1,0:T(8,128)(2,1)S(1)}, u32[]{:S(2)}, u32[]{:S(2)}) collective-permute-start(bf16[384,1536]{1,0:T(8,128)(2,1)S(1)} %get-tuple-element.217), channel_id=1, source_target_pairs={{0,2},{2,0},{4,6},{6,4},{8,10},{10,8},{12,14},{14,12},{16,18},{18,... | collective-permute-start | bytes 3538952 | tf_op jit(solution)/shard_map/ppermute | solution.py:739
  68.3 26.0 %copy-start.3 = (bf16[1024,768]{1,0:T(8,128)(2,1)}, bf16[1024,768]{1,0:T(8,128)(2,1)S(1)}, u32[]{:S(2)}) copy-start(bf16[1024,768]{1,0:T(8,128)(2,1)S(1)} %collective-permute-done.8.other_ref) | copy-start | bytes 4718596
  94.3 5.4 %copy-start.25 = (bf16[768,1536]{1,0:T(8,128)(2,1)S(1)}, bf16[768,1536]{1,0:T(8,128)(2,1)}, u32[]{:S(2)}) copy-start(bf16[768,1536]{1,0:T(8,128)(2,1)} %get-tuple-element.135) | copy-start | bytes 7077892
  94.9 4.8 %collective-permute-start.10 = (bf16[768,1536]{1,0:T(8,128)(2,1)}, bf16[768,1536]{1,0:T(8,128)(2,1)S(1)}, u32[]{:S(2)}, u32[]{:S(2)}) collective-permute-start(bf16[768,1536]{1,0:T(8,128)(2,1)} %get-tuple-element.136), channel_id=1, source_target_pairs={{0,1},{1,0},{2,3},{3,2},{4,5},{5,4},{6,7},{7,6},{8,9},{9,8},{10,11... | collective-permute-start | bytes 7077896 | tf_op jit(solution)/shard_map/ppermute | solution.py:726
  95.0 32.6 %collective-permute-start.11 = (bf16[192,1536]{1,0:T(8,128)(2,1)S(1)}, bf16[192,1536]{1,0:T(8,128)(2,1)S(1)}, u32[]{:S(2)}, u32[]{:S(2)}) collective-permute-start(bf16[192,1536]{1,0:T(8,128)(2,1)S(1)} %get-tuple-element.219), channel_id=1, source_target_pairs={{0,4},{2,6},{4,0},{6,2},{8,12},{10,14},{12,8},{14,10},{16,20},{18,... | collective-permute-start | bytes 1769480 | tf_op jit(solution)/shard_map/ppermute | solution.py:739
  100.4 28.1 %collective-permute-start.12 = (bf16[384,1536]{1,0:T(8,128)(2,1)S(1)}, bf16[384,1536]{1,0:T(8,128)(2,1)S(1)}, u32[]{:S(2)}, u32[]{:S(2)}) collective-permute-start(bf16[384,1536]{1,0:T(8,128)(2,1)S(1)} %get-tuple-element.215), channel_id=1, source_target_pairs={{0,2},{2,0},{4,6},{6,4},{8,10},{10,8},{12,14},{14,12},{16,18},{18,... | collective-permute-start | bytes 3538952 | tf_op jit(solution)/shard_map/ppermute | solution.py:739
  102.2 26.0 %copy-start.27 = (s32[8]{0:T(128)S(1)}, s32[8]{0:T(128)}, u32[]{:S(2)}) copy-start(s32[8]{0:T(128)} %constant.98.clone) | copy-start | bytes 100
  127.5 4.4 %copy-start.29 = (f32[16,768]{1,0:T(8,128)S(1)}, f32[16,768]{1,0:T(8,128)}, u32[]{:S(2)}) copy-start(f32[16,768]{1,0:T(8,128)} %get-tuple-element.164) | copy-start | bytes 147460
  127.5 5.7 %copy-start.5 = (bf16[768,768]{1,0:T(8,128)(2,1)S(1)}, bf16[768,768]{1,0:T(8,128)(2,1)}, u32[]{:S(2)}) copy-start(bf16[768,768]{1,0:T(8,128)(2,1)} %get-tuple-element.156.refs_1_) | copy-start | bytes 3538948
  127.5 5.7 %copy-start.6 = (bf16[768,768]{1,0:T(8,128)(2,1)S(1)}, bf16[768,768]{1,0:T(8,128)(2,1)}, u32[]{:S(2)}) copy-start(bf16[768,768]{1,0:T(8,128)(2,1)} %get-tuple-element.159.refs_3_) | copy-start | bytes 3538948
  127.6 5.7 %copy-start.22 = (f32[16,768]{1,0:T(8,128)S(1)}, f32[16,768]{1,0:T(8,128)}, u32[]{:S(2)}) copy-start(f32[16,768]{1,0:T(8,128)} %get-tuple-element.162.refs_5_) | copy-start | bytes 147460
  127.6 5.6 %collective-permute-start.14 = (bf16[768,768]{1,0:T(8,128)(2,1)}, bf16[768,768]{1,0:T(8,128)(2,1)S(1)}, u32[]{:S(2)}, u32[]{:S(2)}) collective-permute-start(bf16[768,768]{1,0:T(8,128)(2,1)} %get-tuple-element.161), channel_id=1, source_target_pairs={{0,1},{1,0},{2,3},{3,2},{4,5},{5,4},{6,7},{7,6},{8,9},{9,8},{10,11... | collective-permute-start | bytes 3538952 | tf_op jit(solution)/shard_map/ppermute | solution.py:726
  127.7 5.6 %collective-permute-start.13 = (bf16[768,768]{1,0:T(8,128)(2,1)}, bf16[768,768]{1,0:T(8,128)(2,1)S(1)}, u32[]{:S(2)}, u32[]{:S(2)}) collective-permute-start(bf16[768,768]{1,0:T(8,128)(2,1)} %get-tuple-element.158), channel_id=1, source_target_pairs={{0,1},{1,0},{2,3},{3,2},{4,5},{5,4},{6,7},{7,6},{8,9},{9,8},{10,11... | collective-permute-start | bytes 3538952 | tf_op jit(solution)/shard_map/ppermute | solution.py:726
  130.1 5.2 %copy-start.16 = (bf16[192,1536]{1,0:T(8,128)(2,1)}, bf16[192,1536]{1,0:T(8,128)(2,1)S(1)}, u32[]{:S(2)}) copy-start(bf16[192,1536]{1,0:T(8,128)(2,1)S(1)} %get-tuple-element.201) | copy-start | bytes 1769476
  130.1 9.8 %collective-permute-start.16 = (bf16[96,1536]{1,0:T(8,128)(2,1)S(1)}, bf16[96,1536]{1,0:T(8,128)(2,1)}, u32[]{:S(2)}, u32[]{:S(2)}) collective-permute-start(bf16[96,1536]{1,0:T(8,128)(2,1)S(1)} %get-tuple-element.155), channel_id=1, source_target_pairs={{0,8},{2,10},{4,12},{6,14},{8,0},{10,2},{12,4},{14,6},{16,24},{18,... | collective-permute-start | bytes 884744 | tf_op jit(solution)/shard_map/ppermute | solution.py:739
  132.0 1.2 collective-permute-start.15
  133.2 14.1 %copy-start.1 = (f32[1024,768]{1,0:T(8,128)S(1)}, f32[1024,768]{1,0:T(8,128)}, u32[]{:S(2)}) copy-start(f32[1024,768]{1,0:T(8,128)} %get-tuple-element.167.first_ref) | copy-start | bytes 9437188
  137.0 17.0 %collective-permute-start.17 = (bf16[400,768]{1,0:T(8,128)(2,1)}, bf16[400,768]{1,0:T(8,128)(2,1)}, u32[]{:S(2)}, u32[]{:S(2)}) collective-permute-start(bf16[400,768]{1,0:T(8,128)(2,1)} %get-tuple-element.165), channel_id=1, source_target_pairs={{0,2},{2,0},{4,6},{6,4},{8,10},{10,8},{12,14},{14,12},{16,18},{18,... | collective-permute-start | bytes 1843208 | tf_op jit(solution)/shard_map/ppermute | solution.py:739
  138.5 15.5 %collective-permute-start.18 = (bf16[384,768]{1,0:T(8,128)(2,1)}, bf16[384,768]{1,0:T(8,128)(2,1)}, u32[]{:S(2)}, u32[]{:S(2)}) collective-permute-start(bf16[384,768]{1,0:T(8,128)(2,1)} %get-tuple-element.175), channel_id=1, source_target_pairs={{0,4},{2,6},{4,0},{6,2},{8,12},{10,14},{12,8},{14,10},{16,20},{18,... | collective-permute-start | bytes 1769480 | tf_op jit(solution)/shard_map/ppermute | solution.py:739
  140.0 18.8 %collective-permute-start.24 = (bf16[192,1536]{1,0:T(8,128)(2,1)}, bf16[192,1536]{1,0:T(8,128)(2,1)}, u32[]{:S(2)}, u32[]{:S(2)}) collective-permute-start(bf16[192,1536]{1,0:T(8,128)(2,1)} %get-tuple-element.203), channel_id=1, source_target_pairs={{0,8},{2,10},{4,12},{6,14},{8,0},{10,2},{12,4},{14,6},{16,24},{18,... | collective-permute-start | bytes 1769480 | tf_op jit(solution)/shard_map/ppermute | solution.py:739
  142.1 1.4 copy-start.4
  143.5 3.9 %copy-start = (bf16[1024,2304]{1,0:T(8,128)(2,1)S(1)}, bf16[1024,2304]{1,0:T(8,128)(2,1)}, u32[]{:S(2)}) copy-start(bf16[1024,2304]{1,0:T(8,128)(2,1)} %get-tuple-element.171.packed_ref) | copy-start | bytes 14155780
  143.5 3.9 %copy-start.7 = (bf16[768,384]{1,0:T(8,128)(2,1)S(1)}, bf16[768,384]{1,0:T(8,128)(2,1)}, u32[]{:S(2)}) copy-start(bf16[768,384]{1,0:T(8,128)(2,1)} %wq0.3) | copy-start | bytes 1769476
  143.5 3.9 %copy-start.8 = (bf16[768,384]{1,0:T(8,128)(2,1)S(1)}, bf16[768,384]{1,0:T(8,128)(2,1)}, u32[]{:S(2)}) copy-start(bf16[768,384]{1,0:T(8,128)(2,1)} %wk0.3) | copy-start | bytes 1769476
  143.5 4.1 %copy-start.9 = (bf16[768,384]{1,0:T(8,128)(2,1)S(1)}, bf16[768,384]{1,0:T(8,128)(2,1)}, u32[]{:S(2)}) copy-start(bf16[768,384]{1,0:T(8,128)(2,1)} %wv0.3) | copy-start | bytes 1769476
  143.5 4.3 %copy-start.11 = (bf16[768,384]{1,0:T(8,128)(2,1)S(1)}, bf16[768,384]{1,0:T(8,128)(2,1)}, u32[]{:S(2)}) copy-start(bf16[768,384]{1,0:T(8,128)(2,1)} %copy-done.10) | copy-start | bytes 1769476
  149.9 4.1 %copy-start.19 = (bf16[384,768]{1,0:T(8,128)(2,1)S(1)}, bf16[384,768]{1,0:T(8,128)(2,1)}, u32[]{:S(2)}) copy-start(bf16[384,768]{1,0:T(8,128)(2,1)} %copy-done.18) | copy-start | bytes 1769476
  149.9 4.1 %copy-start.21 = (bf16[384,768]{1,0:T(8,128)(2,1)S(1)}, bf16[384,768]{1,0:T(8,128)(2,1)}, u32[]{:S(2)}) copy-start(bf16[384,768]{1,0:T(8,128)(2,1)} %copy-done.20) | copy-start | bytes 1769476
  154.0 4.8 %copy-start.17 = (bf16[192,1536]{1,0:T(8,128)(2,1)S(1)}, bf16[192,1536]{1,0:T(8,128)(2,1)}, u32[]{:S(2)}) copy-start(bf16[192,1536]{1,0:T(8,128)(2,1)} %copy-done.16) | copy-start | bytes 1769476
  156.1 10.1 %collective-permute-start.19 = (bf16[208,768]{1,0:T(8,128)(2,1)S(1)}, bf16[208,768]{1,0:T(8,128)(2,1)S(1)}, u32[]{:S(2)}, u32[]{:S(2)}) collective-permute-start(bf16[208,768]{1,0:T(8,128)(2,1)S(1)} %get-tuple-element.177), channel_id=1, source_target_pairs={{0,4},{2,6},{4,0},{6,2},{8,12},{10,14},{12,8},{14,10},{16,20},{18,... | collective-permute-start | bytes 958472 | tf_op jit(solution)/shard_map/ppermute | solution.py:739
  157.7 7.5 %collective-permute-start.20 = (bf16[192,768]{1,0:T(8,128)(2,1)S(1)}, bf16[192,768]{1,0:T(8,128)(2,1)S(1)}, u32[]{:S(2)}, u32[]{:S(2)}) collective-permute-start(bf16[192,768]{1,0:T(8,128)(2,1)S(1)} %get-tuple-element.181), channel_id=1, source_target_pairs={{0,2},{2,0},{4,6},{6,4},{8,10},{10,8},{12,14},{14,12},{16,18},{18,... | collective-permute-start | bytes 884744 | tf_op jit(solution)/shard_map/ppermute | solution.py:739
  158.8 21.6 %collective-permute-start.22 = (bf16[1024,768]{1,0:T(8,128)(2,1)S(1)}, bf16[1024,768]{1,0:T(8,128)(2,1)S(1)}, u32[]{:S(2)}, u32[]{:S(2)}) collective-permute-start(bf16[1024,768]{1,0:T(8,128)(2,1)S(1)} %tokens_backward.1.own_ref), channel_id=1, source_target_pairs={{0,1},{1,0},{2,3},{3,2},{4,5},{5,4},{6,7},{7,6},{8,9},{9,8},{10,11... | collective-permute-start | bytes 4718600 | tf_op jit(solution)/shard_map/ppermute | solution.py:726
  160.0 11.0 %collective-permute-start.25 = (bf16[96,1536]{1,0:T(8,128)(2,1)S(1)}, bf16[96,1536]{1,0:T(8,128)(2,1)S(1)}, u32[]{:S(2)}, u32[]{:S(2)}) collective-permute-start(bf16[96,1536]{1,0:T(8,128)(2,1)S(1)} %get-tuple-element.221), channel_id=1, source_target_pairs={{0,4},{2,6},{4,0},{6,2},{8,12},{10,14},{12,8},{14,10},{16,20},{18,... | collective-permute-start | bytes 884744 | tf_op jit(solution)/shard_map/ppermute | solution.py:739
  160.6 13.2 %collective-permute-start.27 = (bf16[48,1536]{1,0:T(8,128)(2,1)S(1)}, bf16[48,1536]{1,0:T(8,128)(2,1)S(1)}, u32[]{:S(2)}, u32[]{:S(2)}) collective-permute-start(bf16[48,1536]{1,0:T(8,128)(2,1)S(1)} %get-tuple-element.223), channel_id=1, source_target_pairs={{0,16},{2,18},{4,20},{6,22},{8,24},{10,26},{12,28},{14,30},{16,0},... | collective-permute-start | bytes 442376 | tf_op jit(solution)/shard_map/ppermute | solution.py:739
  166.9 12.0 %collective-permute-start.21 = (bf16[208,768]{1,0:T(8,128)(2,1)S(1)}, bf16[208,768]{1,0:T(8,128)(2,1)S(1)}, u32[]{:S(2)}, u32[]{:S(2)}) collective-permute-start(bf16[208,768]{1,0:T(8,128)(2,1)S(1)} %get-tuple-element.184), channel_id=1, source_target_pairs={{0,8},{2,10},{4,12},{6,14},{8,0},{10,2},{12,4},{14,6},{16,24},{18,... | collective-permute-start | bytes 958472 | tf_op jit(solution)/shard_map/ppermute | solution.py:739
  171.1 8.5 %collective-permute-start.26 = (bf16[48,1536]{1,0:T(8,128)(2,1)S(1)}, bf16[48,1536]{1,0:T(8,128)(2,1)S(1)}, u32[]{:S(2)}, u32[]{:S(2)}) collective-permute-start(bf16[48,1536]{1,0:T(8,128)(2,1)S(1)} %get-tuple-element.225), channel_id=1, source_target_pairs={{0,16},{2,18},{4,20},{6,22},{8,24},{10,26},{12,28},{14,30},{16,0},... | collective-permute-start | bytes 442376 | tf_op jit(solution)/shard_map/ppermute | solution.py:739
  179.5 7.6 %collective-permute-start.23 = (bf16[112,768]{1,0:T(8,128)(2,1)S(1)}, bf16[112,768]{1,0:T(8,128)(2,1)S(1)}, u32[]{:S(2)}, u32[]{:S(2)}) collective-permute-start(bf16[112,768]{1,0:T(8,128)(2,1)S(1)} %get-tuple-element.186), channel_id=1, source_target_pairs={{0,16},{2,18},{4,20},{6,22},{8,24},{10,26},{12,28},{14,30},{16,0},... | collective-permute-start | bytes 516104 | tf_op jit(solution)/shard_map/ppermute | solution.py:739
  (12 other events, 12.7 us)

commit v2 on v1

--- a/solution.py
+++ b/solution.py
@@ -630,7 +630,7 @@
         ),
         name="join_rows",
         **settings(1e6, 4),
-    )(place[0], own, other)
+    )(place[0], *[pltpu.with_memory_space_constraint(v, pltpu.HBM) for v in (own, other)])
 
 
 def exchange_kernel(mine_ref, *refs, chains, small, count, merge, step):

time: 189 us -> 189 us (level)
  waiting for transfers between devices: 20.2 us -> 22.3 us
  Pallas kernels: 118 us -> 120 us
    ppermute x14, waiting for transfers between devices: 15 us -> 17.1 us  [swap_dp(): return lax.ppermute(value, 'dp', [(i, i ^ bit) for i in range(count)])]
    pallas_call x2, Pallas kernels: 3.88 us -> 5.87 us  [join_rows(): pl.pallas_call(join_kernel, out_shape=shape((2 * own.shape[0], D), own.dt...]
  transfers between devices with their start and end apart: 28 -> 28, of which waited for: 10 -> 11; matrix products, arithmetic and copies ran while one was open for 5% -> 4% of each run, Pallas kernels for 49% -> 50%
where the time goes in v2:
time: 189 us; the launch traced here: 188 us
  Pallas kernels  120 us (63%)
  starting transfers between devices  24.6 us (13%)
  waiting for transfers between devices  22.3 us (12%)
  local copies, waits for them, and re-layouts  14 us (7%)
  other arithmetic  6.27 us (3%)
    pallas_call x1, Pallas kernels, ffn_forward(): pl.pallas_call(lambda *refs: ffn_forward_kernel(*refs, chunk=chunk, place...  25.8 us
    pallas_call x1, Pallas kernels, ffn_backward(): pl.pallas_call(lambda *refs: ffn_backward_kernel(*refs, chunk=chunk, plac...  25.7 us
    pallas_call x1, Pallas kernels, attention_backward(): pl.pallas_call(lambda *refs: attention_backward_kernel(*refs, places_a=pl...  25.3 us
    pallas_call x1, Pallas kernels, attention_forward(): pl.pallas_call(attention_forward_kernel, out_shape=(shape((rows, steps *...  21.6 us
    ppermute x14, starting transfers between devices, swap_dp(): return lax.ppermute(value, 'dp', [(i, i ^ bit) for i in range(count)])  21.3 us
    ppermute x14, waiting for transfers between devices, swap_dp(): return lax.ppermute(value, 'dp', [(i, i ^ bit) for i in range(count)])  17.1 us
    unnamed x66, local copies, waits for them, and re-layouts  13.3 us
    pallas_call x5, Pallas kernels, exchange(): pl.pallas_call(lambda *refs: exchange_kernel(*refs, chains=chains, small=...  7.14 us
  transfers between devices with their start and end apart: 28, of which 11 were waited for; matrix products, arithmetic and copies ran while one was open for 4% of the time, Pallas kernels for 50%

profile of v2, /device:TPU:0, one launch (start us, length us, event | category | flops | bytes accessed | tf_op | source)
XLA Modules:
  0.0 188.2 jit_solution(13545887782287822637)
XLA Ops:
  1.8 0.7 constant_dynamic-update-slice_fusion.2
  2.5 0.7 constant_dynamic-update-slice_fusion.1
  3.1 0.7 constant_dynamic-update-slice_fusion.bias0.refs_6_
  4.3 1.1 collective-permute-done.3.bias1.refs_7_
  7.1 21.6 %attention_forward.1 = (bf16[1024,2304]{1,0:T(8,128)(2,1)}, bf16[1024,768]{1,0:T(8,128)(2,1)}, f32[1024,768]{1,0:T(8,128)}, bf16[3,4,512,512]{3,2,1,0:T(8,128)(2...) custom-call(s32[1]{0:T(128)} %bitcast.side_ref.refs_0_, ...), custom_call_target="tpu_custom_call" | custom-call | flops 40000000000 | bytes 1000000 | tf_op jit(solution)/shard_map/attention_forward/pallas_call | solution.py:176
  28.8 1.4 copy-done.28
  30.1 25.8 %ffn_forward.1 = (bf16[1024,1536]{1,0:T(8,128)(2,1)}, bf16[1024,1536]{1,0:T(8,128)(2,1)}, bf16[1024,1536]{1,0:T(8,128)(2,1)}, bf16[1024,768]{1,0:T(8,128)(2,1)},...) custom-call(s32[1]{0:T(128)} %bitcast.side_ref.refs_0_, ...), custom_call_target="tpu_custom_call" | custom-call | flops 40000000000 | bytes 1000000 | tf_op jit(solution)/shard_map/ffn_forward/pallas_call | solution.py:315
  56.5 1.9 %copy-done.21 = bf16[1024,1536]{1,0:T(8,128)(2,1)S(1)} copy-done((bf16[1024,1536]{1,0:T(8,128)(2,1)S(1)}, bf16[1024,1536]{1,0:T(8,128)(2,1)}, u32[]{:S(2)}) %copy-start.21) | copy-done | bytes 3145752
  58.4 1.4 copy-done.22
  59.8 3.4 %outer_weight.1 = bf16[768,1536]{1,0:T(8,128)(2,1)S(1)} custom-call(bf16[1024,768]{1,0:T(8,128)(2,1)S(1)} %copy-done.22, bf16[1024,1536]{1,0:T(8,128)(2,1)S(1)} %copy-done.21), custom_call_target="tpu_custom_call" | custom-call | flops 10000000000 | bytes 1000000 | tf_op jit(solution)/shard_map/outer_weight/pallas_call | solution.py:346
  63.8 2.9 %collective-permute-start.9 = (bf16[384,1536]{1,0:T(8,128)(2,1)S(1)}, bf16[384,1536]{1,0:T(8,128)(2,1)S(1)}, u32[]{:S(2)}, u32[]{:S(2)}) collective-permute-start(bf16[384,1536]{1,0:T(8,128)(2,1)S(1)} %get-tuple-element.217), channel_id=1, source_target_pairs={{0,2},{2,0},{4,6},{6,4},{8,10},{10,8},{12,14},{14,12},{16,18},{18,... | collective-permute-start | bytes 3538952 | tf_op jit(solution)/shard_map/ppermute | solution.py:739
  66.7 25.7 %ffn_backward.1 = (bf16[768,1536]{1,0:T(8,128)(2,1)}, bf16[768,1536]{1,0:T(8,128)(2,1)}, f32[8,1536]{1,0:T(8,128)}, f32[8,1536]{1,0:T(8,128)}, f32[1024,768]{1,0...) custom-call(bf16[1024,768]{1,0:T(8,128)(2,1)} %get-tuple-element.123.refs_0_, ...), custom_call_target="tpu_custom_call" | custom-call | flops 40000000000 | bytes 1000000 | tf_op jit(solution)/shard_map/ffn_backward/pallas_call | solution.py:433
  93.4 1.8 collective-permute-start.11
  95.2 2.9 %collective-permute-done.10 = bf16[768,1536]{1,0:T(8,128)(2,1)S(1)} collective-permute-done((bf16[768,1536]{1,0:T(8,128)(2,1)}, bf16[768,1536]{1,0:T(8,128)(2,1)S(1)}, u32[]{:S(2)}, u32[]{:S(2)}) %collective-permute-start.10) | collective-permute-done | bytes 2359328 | tf_op jit(solution)/shard_map/ppermute | solution.py:726
  98.7 1.8 collective-permute-start.12
  100.6 25.3 %attention_backward.1 = (bf16[1024,2304]{1,0:T(8,128)(2,1)}, bf16[768,768]{1,0:T(8,128)(2,1)}, bf16[768,768]{1,0:T(8,128)(2,1)}, bf16[768,768]{1,0:T(8,128)(2,1)...) custom-call(s32[1]{0:T(128)} %bitcast.side_ref.refs_0_, bf16[2048,768]{1,0:T(8,128)(2,1)} %refs_2_.3, ...), custom_call_target="tpu_custom_call" | custom-call | flops 1000000 | bytes 1000000 | tf_op jit(solution)/shard_map/attention_backward/pallas_call | solution.py:544
  126.8 1.7 exchange.5
  128.5 1.8 collective-permute-start.16
  130.4 1.2 collective-permute-done.15.refs_6_
  131.7 2.0 %exchange.6 = (bf16[400,768]{1,0:T(8,128)(2,1)}, bf16[384,768]{1,0:T(8,128)(2,1)S(1)}, bf16[384,768]{1,0:T(8,128)(2,1)}, bf16[384,768]{1,0:T(8,128)(2,1)S(1)}, f32[16,768]{1,0:T(8,128)S(1)}) custom-call(s32[8]{0:T(128)S(1)} %and_select_fusion.refs_0_, bf16[768,768]{1,0:T(8,128)(2,1)S(1)} %copy-done.3, bf16[768,768]{1,0:T(8,128)(2,1)S(1)} %collective-permute-done.13.refs_2_, ...), custom_call_target="tpu_custom_call" | custom-call | flops 1000000 | bytes 1000000 | tf_op jit(solution)/shard_map/exchange/pallas_call | solution.py:672
  133.7 0.8 copy-done.16
  134.5 0.9 copy-done.18
  135.4 1.5 collective-permute-start.17
  136.9 1.5 collective-permute-start.18
  138.4 0.7 copy-done.26
  139.7 3.0 %join_rows.2 = bf16[2048,768]{1,0:T(8,128)(2,1)} custom-call(s32[1]{0:T(128)} %bitcast.side_ref.refs_0_, bf16[1024,768]{1,0:T(8,128)(2,1)} %get-tuple-element.166.own_ref, bf16[1024,768]{1,0:T(8,128)(2,1)} %collective-permute-done.8.other_ref), custom_call_target="tpu_custom_call" | custom-call | flops 1000000 | bytes 1000000 | tf_op jit(solution)/shard_map/join_rows/pallas_call | solution.py:617
  142.7 1.9 add_convert_fusion.8
  144.9 1.1 copy-done.11
  146.0 1.1 copy-done.13
  147.1 4.3 %tokens_backward.1.own_ref = bf16[1024,768]{1,0:T(8,128)(2,1)S(1)} custom-call(f32[1024,768]{1,0:T(8,128)S(1)} %copy-done.2, bf16[1024,2304]{1,0:T(8,128)(2,1)S(1)} %copy-done.1, bf16[768,384]{1,0:T(8,128)(2,1)S(1)} %copy-done.5, bf16[768,384]{1,0:T(8,128)(2,1)S(1)} %copy-done.9, bf16[768,384]{1,0:T(8,128)(2,1)S(1)} %copy-done.6, ...), custom_call_target="tpu_custom_call" | custom-call | flops 1000000 | bytes 1000000 | tf_op jit(solution)/shard_map/tokens_backward/pallas_call | solution.py:583
  151.4 0.9 collective-permute-done.18.refs_4_
  152.3 2.1 %exchange.7 = (bf16[208,768]{1,0:T(8,128)(2,1)S(1)}, bf16[192,768]{1,0:T(8,128)(2,1)S(1)}, bf16[192,768]{1,0:T(8,128)(2,1)S(1)}, bf16[192,768]{1,0:T(8,128)(2,1)S(1)}, f32[16,768]{1,0:T(8,128)S(1)}) custom-call(s32[8]{0:T(128)S(1)} %and_select_fusion.refs_0_, bf16[384,768]{1,0:T(8,128)(2,1)S(1)} %copy-done.17, ...), custom_call_target="tpu_custom_call" | custom-call | flops 1000000 | bytes 1000000 | tf_op jit(solution)/shard_map/exchange/pallas_call | solution.py:672
  154.4 1.6 collective-permute-start.19
  156.0 0.8 collective-permute-start.20
  156.8 1.2 add_convert_fusion.7
  158.6 2.6 %collective-permute-start.27 = (bf16[48,1536]{1,0:T(8,128)(2,1)S(1)}, bf16[48,1536]{1,0:T(8,128)(2,1)S(1)}, u32[]{:S(2)}, u32[]{:S(2)}) collective-permute-start(bf16[48,1536]{1,0:T(8,128)(2,1)S(1)} %get-tuple-element.223), channel_id=1, source_target_pairs={{0,16},{2,18},{4,20},{6,22},{8,24},{10,26},{12,28},{14,30},{16,0},... | collective-permute-start | bytes 442376 | tf_op jit(solution)/shard_map/ppermute | solution.py:739
  161.1 2.5 %collective-permute-done.20.refs_4_ = bf16[192,768]{1,0:T(8,128)(2,1)S(1)} collective-permute-done((bf16[192,768]{1,0:T(8,128)(2,1)S(1)}, bf16[192,768]{1,0:T(8,128)(2,1)S(1)}, u32[]{:S(2)}, u32[]{:S(2)}) %collective-permute-start.20) | collective-permute-done | bytes 294944 | tf_op jit(solution)/shard_map/ppermute | solution.py:739
  163.6 1.0 collective-permute-done.19.refs_2_
  165.3 1.1 collective-permute-start.21
  166.4 2.8 %collective-permute-done.25 = bf16[96,1536]{1,0:T(8,128)(2,1)S(1)} collective-permute-done((bf16[96,1536]{1,0:T(8,128)(2,1)S(1)}, bf16[96,1536]{1,0:T(8,128)(2,1)S(1)}, u32[]{:S(2)}, u32[]{:S(2)}) %collective-permute-start.25) | collective-permute-done | bytes 294944 | tf_op jit(solution)/shard_map/ppermute | solution.py:739
  169.3 2.7 %collective-permute-start.26 = (bf16[48,1536]{1,0:T(8,128)(2,1)S(1)}, bf16[48,1536]{1,0:T(8,128)(2,1)S(1)}, u32[]{:S(2)}, u32[]{:S(2)}) collective-permute-start(bf16[48,1536]{1,0:T(8,128)(2,1)S(1)} %get-tuple-element.225), channel_id=1, source_target_pairs={{0,16},{2,18},{4,20},{6,22},{8,24},{10,26},{12,28},{14,30},{16,0},... | collective-permute-start | bytes 442376 | tf_op jit(solution)/shard_map/ppermute | solution.py:739
  172.0 0.7 add_bitcast_fusion
  172.7 5.2 %collective-permute-done.21.refs_2_ = bf16[208,768]{1,0:T(8,128)(2,1)S(1)} collective-permute-done((bf16[208,768]{1,0:T(8,128)(2,1)S(1)}, bf16[208,768]{1,0:T(8,128)(2,1)S(1)}, u32[]{:S(2)}, u32[]{:S(2)}) %collective-permute-start.21) | collective-permute-done | bytes 319520 | tf_op jit(solution)/shard_map/ppermute | solution.py:739
  178.6 0.7 convert_add_fusion
  179.3 1.2 copy-done.24
  180.5 2.9 %join_rows.3 = bf16[2048,768]{1,0:T(8,128)(2,1)} custom-call(s32[1]{0:T(128)} %bitcast.side_ref.refs_0_, bf16[1024,768]{1,0:T(8,128)(2,1)} %copy-done, bf16[1024,768]{1,0:T(8,128)(2,1)} %copy-done.24), custom_call_target="tpu_custom_call" | custom-call | flops 1000000 | bytes 1000000 | tf_op jit(solution)/shard_map/join_rows/pallas_call | solution.py:617
  183.4 3.9 %collective-permute-done.23.recv_ref = bf16[112,768]{1,0:T(8,128)(2,1)S(1)} collective-permute-done((bf16[112,768]{1,0:T(8,128)(2,1)S(1)}, bf16[112,768]{1,0:T(8,128)(2,1)S(1)}, u32[]{:S(2)}, u32[]{:S(2)}) %collective-permute-start.23) | collective-permute-done | bytes 172064 | tf_op jit(solution)/shard_map/ppermute | solution.py:739
  187.2 0.8 finish.1
  (99 shorter events, 9.9 us)
Async XLA Ops:
  0.7 5.1 %collective-permute-start = (bf16[768,384]{1,0:T(8,128)(2,1)}, bf16[768,384]{1,0:T(8,128)(2,1)S(1)}, u32[]{:S(2)}, u32[]{:S(2)}) collective-permute-start(bf16[768,384]{1,0:T(8,128)(2,1)} %wq0.3), channel_id=1, source_target_pairs={{0,1},{1,0},{2,3},{3,2},{4,5},{5,4},{6,7},{7,6},{8,9},{9,8},{10,11... | collective-permute-start | bytes 1769480 | tf_op jit(solution)/shard_map/ppermute | solution.py:726
  1.2 4.7 %collective-permute-start.1 = (bf16[768,384]{1,0:T(8,128)(2,1)}, bf16[768,384]{1,0:T(8,128)(2,1)S(1)}, u32[]{:S(2)}, u32[]{:S(2)}) collective-permute-start(bf16[768,384]{1,0:T(8,128)(2,1)} %wk0.3), channel_id=1, source_target_pairs={{0,1},{1,0},{2,3},{3,2},{4,5},{5,4},{6,7},{7,6},{8,9},{9,8},{10,11... | collective-permute-start | bytes 1769480 | tf_op jit(solution)/shard_map/ppermute | solution.py:726
  1.3 4.6 %collective-permute-start.2 = (bf16[768,384]{1,0:T(8,128)(2,1)}, bf16[768,384]{1,0:T(8,128)(2,1)S(1)}, u32[]{:S(2)}, u32[]{:S(2)}) collective-permute-start(bf16[768,384]{1,0:T(8,128)(2,1)} %wv0.3), channel_id=1, source_target_pairs={{0,1},{1,0},{2,3},{3,2},{4,5},{5,4},{6,7},{7,6},{8,9},{9,8},{10,11... | collective-permute-start | bytes 1769480 | tf_op jit(solution)/shard_map/ppermute | solution.py:726
  1.7 4.2 %collective-permute-start.4 = (bf16[384,768]{1,0:T(8,128)(2,1)}, bf16[384,768]{1,0:T(8,128)(2,1)S(1)}, u32[]{:S(2)}, u32[]{:S(2)}) collective-permute-start(bf16[384,768]{1,0:T(8,128)(2,1)} %refs_9_.1), channel_id=1, source_target_pairs={{0,1},{1,0},{2,3},{3,2},{4,5},{5,4},{6,7},{7,6},{8,9},{9,8},{10,11... | collective-permute-start | bytes 1769480 | tf_op jit(solution)/shard_map/ppermute | solution.py:726
  3.8 2.1 %copy-start.31 = (f32[2304]{0:T(1024)}, f32[2304]{0:T(1024)S(1)}, u32[]{:S(2)}) copy-start(f32[2304]{0:T(1024)S(1)} %constant_dynamic-update-slice_fusion.bias0.refs_6_) | copy-start | bytes 27652
  3.8 1.5 collective-permute-start.3
  5.4 23.4 %collective-permute-start.5 = (bf16[768,1536]{1,0:T(8,128)(2,1)}, bf16[768,1536]{1,0:T(8,128)(2,1)S(1)}, u32[]{:S(2)}, u32[]{:S(2)}) collective-permute-start(bf16[768,1536]{1,0:T(8,128)(2,1)} %refs_5_.1), channel_id=1, source_target_pairs={{0,1},{1,0},{2,3},{3,2},{4,5},{5,4},{6,7},{7,6},{8,9},{9,8},{10,11... | collective-permute-start | bytes 7077896 | tf_op jit(solution)/shard_map/ppermute | solution.py:726
  5.7 23.0 %collective-permute-start.6 = (bf16[1536,768]{1,0:T(8,128)(2,1)}, bf16[1536,768]{1,0:T(8,128)(2,1)}, u32[]{:S(2)}, u32[]{:S(2)}) collective-permute-start(bf16[1536,768]{1,0:T(8,128)(2,1)} %refs_3_.1), channel_id=1, source_target_pairs={{0,1},{1,0},{2,3},{3,2},{4,5},{5,4},{6,7},{7,6},{8,9},{9,8},{10,11... | collective-permute-start | bytes 7077896 | tf_op jit(solution)/shard_map/ppermute | solution.py:726
  55.9 7.3 %collective-permute-start.7 = (bf16[768,1536]{1,0:T(8,128)(2,1)}, bf16[768,1536]{1,0:T(8,128)(2,1)S(1)}, u32[]{:S(2)}, u32[]{:S(2)}) collective-permute-start(bf16[768,1536]{1,0:T(8,128)(2,1)} %get-tuple-element.121), channel_id=1, source_target_pairs={{0,1},{1,0},{2,3},{3,2},{4,5},{5,4},{6,7},{7,6},{8,9},{9,8},{10,11... | collective-permute-start | bytes 7077896 | tf_op jit(solution)/shard_map/ppermute | solution.py:726
  56.3 10.4 %collective-permute-start.8 = (bf16[1024,768]{1,0:T(8,128)(2,1)}, bf16[1024,768]{1,0:T(8,128)(2,1)}, u32[]{:S(2)}, u32[]{:S(2)}) collective-permute-start(bf16[1024,768]{1,0:T(8,128)(2,1)} %get-tuple-element.166.own_ref), channel_id=1, source_target_pairs={{0,1},{1,0},{2,3},{3,2},{4,5},{5,4},{6,7},{7,6},{8,9},{9,8},{10,11... | collective-permute-start | bytes 4718600 | tf_op jit(solution)/shard_map/ppermute | solution.py:726
  56.5 1.9 %copy-start.21 = (bf16[1024,1536]{1,0:T(8,128)(2,1)S(1)}, bf16[1024,1536]{1,0:T(8,128)(2,1)}, u32[]{:S(2)}) copy-start(bf16[1024,1536]{1,0:T(8,128)(2,1)} %get-tuple-element.120.refs_1_) | copy-start | bytes 9437188
  58.4 1.4 copy-start.22
  63.8 29.2 %collective-permute-start.9 = (bf16[384,1536]{1,0:T(8,128)(2,1)S(1)}, bf16[384,1536]{1,0:T(8,128)(2,1)S(1)}, u32[]{:S(2)}, u32[]{:S(2)}) collective-permute-start(bf16[384,1536]{1,0:T(8,128)(2,1)S(1)} %get-tuple-element.217), channel_id=1, source_target_pairs={{0,2},{2,0},{4,6},{6,4},{8,10},{10,8},{12,14},{14,12},{16,18},{18,... | collective-permute-start | bytes 3538952 | tf_op jit(solution)/shard_map/ppermute | solution.py:739
  92.4 5.8 %copy-start.23 = (bf16[768,1536]{1,0:T(8,128)(2,1)S(1)}, bf16[768,1536]{1,0:T(8,128)(2,1)}, u32[]{:S(2)}) copy-start(bf16[768,1536]{1,0:T(8,128)(2,1)} %get-tuple-element.135) | copy-start | bytes 7077892
  93.3 4.8 %collective-permute-start.10 = (bf16[768,1536]{1,0:T(8,128)(2,1)}, bf16[768,1536]{1,0:T(8,128)(2,1)S(1)}, u32[]{:S(2)}, u32[]{:S(2)}) collective-permute-start(bf16[768,1536]{1,0:T(8,128)(2,1)} %get-tuple-element.136), channel_id=1, source_target_pairs={{0,1},{1,0},{2,3},{3,2},{4,5},{5,4},{6,7},{7,6},{8,9},{9,8},{10,11... | collective-permute-start | bytes 7077896 | tf_op jit(solution)/shard_map/ppermute | solution.py:726
  93.4 32.6 %collective-permute-start.11 = (bf16[192,1536]{1,0:T(8,128)(2,1)S(1)}, bf16[192,1536]{1,0:T(8,128)(2,1)S(1)}, u32[]{:S(2)}, u32[]{:S(2)}) collective-permute-start(bf16[192,1536]{1,0:T(8,128)(2,1)S(1)} %get-tuple-element.219), channel_id=1, source_target_pairs={{0,4},{2,6},{4,0},{6,2},{8,12},{10,14},{12,8},{14,10},{16,20},{18,... | collective-permute-start | bytes 1769480 | tf_op jit(solution)/shard_map/ppermute | solution.py:739
  98.7 28.1 %collective-permute-start.12 = (bf16[384,1536]{1,0:T(8,128)(2,1)S(1)}, bf16[384,1536]{1,0:T(8,128)(2,1)S(1)}, u32[]{:S(2)}, u32[]{:S(2)}) collective-permute-start(bf16[384,1536]{1,0:T(8,128)(2,1)S(1)} %get-tuple-element.215), channel_id=1, source_target_pairs={{0,2},{2,0},{4,6},{6,4},{8,10},{10,8},{12,14},{14,12},{16,18},{18,... | collective-permute-start | bytes 3538952 | tf_op jit(solution)/shard_map/ppermute | solution.py:739
  100.6 26.0 %copy-start.27 = (s32[8]{0:T(128)S(1)}, s32[8]{0:T(128)}, u32[]{:S(2)}) copy-start(s32[8]{0:T(128)} %constant.98.clone) | copy-start | bytes 100
  125.9 4.5 %copy-start.29 = (f32[16,768]{1,0:T(8,128)S(1)}, f32[16,768]{1,0:T(8,128)}, u32[]{:S(2)}) copy-start(f32[16,768]{1,0:T(8,128)} %get-tuple-element.164) | copy-start | bytes 147460
  125.9 5.7 %copy-start.3 = (bf16[768,768]{1,0:T(8,128)(2,1)S(1)}, bf16[768,768]{1,0:T(8,128)(2,1)}, u32[]{:S(2)}) copy-start(bf16[768,768]{1,0:T(8,128)(2,1)} %get-tuple-element.156.refs_1_) | copy-start | bytes 3538948
  125.9 5.7 %copy-start.4 = (bf16[768,768]{1,0:T(8,128)(2,1)S(1)}, bf16[768,768]{1,0:T(8,128)(2,1)}, u32[]{:S(2)}) copy-start(bf16[768,768]{1,0:T(8,128)(2,1)} %get-tuple-element.159.refs_3_) | copy-start | bytes 3538948
  125.9 5.7 %copy-start.20 = (f32[16,768]{1,0:T(8,128)S(1)}, f32[16,768]{1,0:T(8,128)}, u32[]{:S(2)}) copy-start(f32[16,768]{1,0:T(8,128)} %get-tuple-element.162.refs_5_) | copy-start | bytes 147460
  126.0 5.7 %collective-permute-start.14 = (bf16[768,768]{1,0:T(8,128)(2,1)}, bf16[768,768]{1,0:T(8,128)(2,1)S(1)}, u32[]{:S(2)}, u32[]{:S(2)}) collective-permute-start(bf16[768,768]{1,0:T(8,128)(2,1)} %get-tuple-element.161), channel_id=1, source_target_pairs={{0,1},{1,0},{2,3},{3,2},{4,5},{5,4},{6,7},{7,6},{8,9},{9,8},{10,11... | collective-permute-start | bytes 3538952 | tf_op jit(solution)/shard_map/ppermute | solution.py:726
  126.0 5.6 %collective-permute-start.13 = (bf16[768,768]{1,0:T(8,128)(2,1)}, bf16[768,768]{1,0:T(8,128)(2,1)S(1)}, u32[]{:S(2)}, u32[]{:S(2)}) collective-permute-start(bf16[768,768]{1,0:T(8,128)(2,1)} %get-tuple-element.158), channel_id=1, source_target_pairs={{0,1},{1,0},{2,3},{3,2},{4,5},{5,4},{6,7},{7,6},{8,9},{9,8},{10,11... | collective-permute-start | bytes 3538952 | tf_op jit(solution)/shard_map/ppermute | solution.py:726
  128.5 5.2 %copy-start.14 = (bf16[192,1536]{1,0:T(8,128)(2,1)}, bf16[192,1536]{1,0:T(8,128)(2,1)S(1)}, u32[]{:S(2)}) copy-start(bf16[192,1536]{1,0:T(8,128)(2,1)S(1)} %get-tuple-element.201) | copy-start | bytes 1769476
  128.5 9.9 %collective-permute-start.16 = (bf16[96,1536]{1,0:T(8,128)(2,1)S(1)}, bf16[96,1536]{1,0:T(8,128)(2,1)S(1)}, u32[]{:S(2)}, u32[]{:S(2)}) collective-permute-start(bf16[96,1536]{1,0:T(8,128)(2,1)S(1)} %get-tuple-element.155), channel_id=1, source_target_pairs={{0,8},{2,10},{4,12},{6,14},{8,0},{10,2},{12,4},{14,6},{16,24},{18,... | collective-permute-start | bytes 884744 | tf_op jit(solution)/shard_map/ppermute | solution.py:739
  130.4 1.2 collective-permute-start.15
  131.6 13.0 %copy-start.2 = (f32[1024,768]{1,0:T(8,128)S(1)}, f32[1024,768]{1,0:T(8,128)}, u32[]{:S(2)}) copy-start(f32[1024,768]{1,0:T(8,128)} %get-tuple-element.167.first_ref) | copy-start | bytes 9437188
  135.4 16.9 %collective-permute-start.17 = (bf16[400,768]{1,0:T(8,128)(2,1)}, bf16[400,768]{1,0:T(8,128)(2,1)}, u32[]{:S(2)}, u32[]{:S(2)}) collective-permute-start(bf16[400,768]{1,0:T(8,128)(2,1)} %get-tuple-element.165), channel_id=1, source_target_pairs={{0,2},{2,0},{4,6},{6,4},{8,10},{10,8},{12,14},{14,12},{16,18},{18,... | collective-permute-start | bytes 1843208 | tf_op jit(solution)/shard_map/ppermute | solution.py:739
  136.9 15.4 %collective-permute-start.18 = (bf16[384,768]{1,0:T(8,128)(2,1)}, bf16[384,768]{1,0:T(8,128)(2,1)}, u32[]{:S(2)}, u32[]{:S(2)}) collective-permute-start(bf16[384,768]{1,0:T(8,128)(2,1)} %get-tuple-element.175), channel_id=1, source_target_pairs={{0,4},{2,6},{4,0},{6,2},{8,12},{10,14},{12,8},{14,10},{16,20},{18,... | collective-permute-start | bytes 1769480 | tf_op jit(solution)/shard_map/ppermute | solution.py:739
  139.1 17.7 %collective-permute-start.24 = (bf16[192,1536]{1,0:T(8,128)(2,1)}, bf16[192,1536]{1,0:T(8,128)(2,1)}, u32[]{:S(2)}, u32[]{:S(2)}) collective-permute-start(bf16[192,1536]{1,0:T(8,128)(2,1)} %get-tuple-element.203), channel_id=1, source_target_pairs={{0,8},{2,10},{4,12},{6,14},{8,0},{10,2},{12,4},{14,6},{16,24},{18,... | collective-permute-start | bytes 1769480 | tf_op jit(solution)/shard_map/ppermute | solution.py:739
  139.7 4.9 %copy-start.1 = (bf16[1024,2304]{1,0:T(8,128)(2,1)S(1)}, bf16[1024,2304]{1,0:T(8,128)(2,1)}, u32[]{:S(2)}) copy-start(bf16[1024,2304]{1,0:T(8,128)(2,1)} %get-tuple-element.171.packed_ref) | copy-start | bytes 14155780
  139.7 4.9 %copy-start.5 = (bf16[768,384]{1,0:T(8,128)(2,1)S(1)}, bf16[768,384]{1,0:T(8,128)(2,1)}, u32[]{:S(2)}) copy-start(bf16[768,384]{1,0:T(8,128)(2,1)} %wq0.3) | copy-start | bytes 1769476
  139.7 4.9 %copy-start.6 = (bf16[768,384]{1,0:T(8,128)(2,1)S(1)}, bf16[768,384]{1,0:T(8,128)(2,1)}, u32[]{:S(2)}) copy-start(bf16[768,384]{1,0:T(8,128)(2,1)} %wk0.3) | copy-start | bytes 1769476
  139.7 5.0 %copy-start.7 = (bf16[768,384]{1,0:T(8,128)(2,1)S(1)}, bf16[768,384]{1,0:T(8,128)(2,1)}, u32[]{:S(2)}) copy-start(bf16[768,384]{1,0:T(8,128)(2,1)} %wv0.3) | copy-start | bytes 1769476
  139.7 5.2 %copy-start.9 = (bf16[768,384]{1,0:T(8,128)(2,1)S(1)}, bf16[768,384]{1,0:T(8,128)(2,1)}, u32[]{:S(2)}) copy-start(bf16[768,384]{1,0:T(8,128)(2,1)} %copy-done.8) | copy-start | bytes 1769476
  147.1 5.3 %copy-start.17 = (bf16[384,768]{1,0:T(8,128)(2,1)S(1)}, bf16[384,768]{1,0:T(8,128)(2,1)}, u32[]{:S(2)}) copy-start(bf16[384,768]{1,0:T(8,128)(2,1)} %copy-done.16) | copy-start | bytes 1769476
  147.1 5.3 %copy-start.19 = (bf16[384,768]{1,0:T(8,128)(2,1)S(1)}, bf16[384,768]{1,0:T(8,128)(2,1)}, u32[]{:S(2)}) copy-start(bf16[384,768]{1,0:T(8,128)(2,1)} %copy-done.18) | copy-start | bytes 1769476
  151.4 13.9 %copy-start = (bf16[1024,768]{1,0:T(8,128)(2,1)}, bf16[1024,768]{1,0:T(8,128)(2,1)S(1)}, u32[]{:S(2)}) copy-start(bf16[1024,768]{1,0:T(8,128)(2,1)S(1)} %tokens_backward.1.own_ref) | copy-start | bytes 4718596
  151.4 5.4 %copy-start.15 = (bf16[192,1536]{1,0:T(8,128)(2,1)S(1)}, bf16[192,1536]{1,0:T(8,128)(2,1)}, u32[]{:S(2)}) copy-start(bf16[192,1536]{1,0:T(8,128)(2,1)} %copy-done.14) | copy-start | bytes 1769476
  154.4 10.2 %collective-permute-start.19 = (bf16[208,768]{1,0:T(8,128)(2,1)S(1)}, bf16[208,768]{1,0:T(8,128)(2,1)S(1)}, u32[]{:S(2)}, u32[]{:S(2)}) collective-permute-start(bf16[208,768]{1,0:T(8,128)(2,1)S(1)} %get-tuple-element.177), channel_id=1, source_target_pairs={{0,4},{2,6},{4,0},{6,2},{8,12},{10,14},{12,8},{14,10},{16,20},{18,... | collective-permute-start | bytes 958472 | tf_op jit(solution)/shard_map/ppermute | solution.py:739
  156.0 7.6 %collective-permute-start.20 = (bf16[192,768]{1,0:T(8,128)(2,1)S(1)}, bf16[192,768]{1,0:T(8,128)(2,1)S(1)}, u32[]{:S(2)}, u32[]{:S(2)}) collective-permute-start(bf16[192,768]{1,0:T(8,128)(2,1)S(1)} %get-tuple-element.181), channel_id=1, source_target_pairs={{0,2},{2,0},{4,6},{6,4},{8,10},{10,8},{12,14},{14,12},{16,18},{18,... | collective-permute-start | bytes 884744 | tf_op jit(solution)/shard_map/ppermute | solution.py:739
  156.8 22.6 %collective-permute-start.22 = (bf16[1024,768]{1,0:T(8,128)(2,1)S(1)}, bf16[1024,768]{1,0:T(8,128)(2,1)S(1)}, u32[]{:S(2)}, u32[]{:S(2)}) collective-permute-start(bf16[1024,768]{1,0:T(8,128)(2,1)S(1)} %tokens_backward.1.own_ref), channel_id=1, source_target_pairs={{0,1},{1,0},{2,3},{3,2},{4,5},{5,4},{6,7},{7,6},{8,9},{9,8},{10,11... | collective-permute-start | bytes 4718600 | tf_op jit(solution)/shard_map/ppermute | solution.py:726
  158.0 11.2 %collective-permute-start.25 = (bf16[96,1536]{1,0:T(8,128)(2,1)S(1)}, bf16[96,1536]{1,0:T(8,128)(2,1)S(1)}, u32[]{:S(2)}, u32[]{:S(2)}) collective-permute-start(bf16[96,1536]{1,0:T(8,128)(2,1)S(1)} %get-tuple-element.221), channel_id=1, source_target_pairs={{0,4},{2,6},{4,0},{6,2},{8,12},{10,14},{12,8},{14,10},{16,20},{18,... | collective-permute-start | bytes 884744 | tf_op jit(solution)/shard_map/ppermute | solution.py:739
  158.6 13.4 %collective-permute-start.27 = (bf16[48,1536]{1,0:T(8,128)(2,1)S(1)}, bf16[48,1536]{1,0:T(8,128)(2,1)S(1)}, u32[]{:S(2)}, u32[]{:S(2)}) collective-permute-start(bf16[48,1536]{1,0:T(8,128)(2,1)S(1)} %get-tuple-element.223), channel_id=1, source_target_pairs={{0,16},{2,18},{4,20},{6,22},{8,24},{10,26},{12,28},{14,30},{16,0},... | collective-permute-start | bytes 442376 | tf_op jit(solution)/shard_map/ppermute | solution.py:739
  165.3 12.6 %collective-permute-start.21 = (bf16[208,768]{1,0:T(8,128)(2,1)S(1)}, bf16[208,768]{1,0:T(8,128)(2,1)S(1)}, u32[]{:S(2)}, u32[]{:S(2)}) collective-permute-start(bf16[208,768]{1,0:T(8,128)(2,1)S(1)} %get-tuple-element.184), channel_id=1, source_target_pairs={{0,8},{2,10},{4,12},{6,14},{8,0},{10,2},{12,4},{14,6},{16,24},{18,... | collective-permute-start | bytes 958472 | tf_op jit(solution)/shard_map/ppermute | solution.py:739
  169.3 9.3 %collective-permute-start.26 = (bf16[48,1536]{1,0:T(8,128)(2,1)S(1)}, bf16[48,1536]{1,0:T(8,128)(2,1)S(1)}, u32[]{:S(2)}, u32[]{:S(2)}) collective-permute-start(bf16[48,1536]{1,0:T(8,128)(2,1)S(1)} %get-tuple-element.225), channel_id=1, source_target_pairs={{0,16},{2,18},{4,20},{6,22},{8,24},{10,26},{12,28},{14,30},{16,0},... | collective-permute-start | bytes 442376 | tf_op jit(solution)/shard_map/ppermute | solution.py:739
  178.5 8.7 %collective-permute-start.23 = (bf16[112,768]{1,0:T(8,128)(2,1)S(1)}, bf16[112,768]{1,0:T(8,128)(2,1)S(1)}, u32[]{:S(2)}, u32[]{:S(2)}) collective-permute-start(bf16[112,768]{1,0:T(8,128)(2,1)S(1)} %get-tuple-element.186), channel_id=1, source_target_pairs={{0,16},{2,18},{4,20},{6,22},{8,24},{10,26},{12,28},{14,30},{16,0},... | collective-permute-start | bytes 516104 | tf_op jit(solution)/shard_map/ppermute | solution.py:739
  (12 other events, 11.7 us)
